TPU v7x, 128 devices: a whole 4x4x4 slice. The times are simulated.
128 devices in a mesh: pool: 2 (over z_hi), dev: 64 (over x, z_lo, y, core).
Axes of the slice: x: 4, y: 4, z: 4 (z_hi: 2, z_lo: 2; z = z_hi * 2 + z_lo), core: 2. Of those that a mesh axis runs over, the one named last changes fastest.
Arguments:
- queries: bfloat16 [2048, 4096], P(('pool', 'dev')), may hold values from -6 to 6
- new_kv: bfloat16 [2048, 512], P(('pool', 'dev')), may hold values from -6 to 6
- kv_pages: bfloat16 [16384, 16, 512], P(('pool', 'dev')), may hold values from -6 to 6
- page_table: int32 [2048, 16], P(('pool', 'dev')), may hold values from 0 to 143, as said below
- lengths: int32 [2048], P(('pool', 'dev')), may hold values from 1 to 256, as said below
- shed_slots: int32 [2048], P(('pool', 'dev')), may hold values from 0 to 127, as said below
- residual: bfloat16 [2048, 4096], P(('pool', 'dev')), may hold values from -6 to 6
- norm_gain: float32 [4096], replicated, may hold values from 0.1 to 1.9
- expert_ids: int32 [2048, 8], P(('pool', 'dev')), may hold values from 0 to 127, all different within a row; in each aligned block of 16 rows (0 to 15, 16 to 31, ...) at most 2 rows name the same one
- gate_weights: float32 [2048, 8], P(('pool', 'dev')), may hold values from 0.05 to 0.6
- w_gate_up: bfloat16 [128, 4096, 1536], P(('pool', 'dev')), may hold values from -0.09375 to 0.09375
- w_down: bfloat16 [128, 768, 4096], P(('pool', 'dev')), may hold values from -0.21875 to 0.21875
Outputs:
- attended: bfloat16 [2048, 4096], P(('pool', 'dev'))
- layer_out: bfloat16 [2048, 4096], P(('pool', 'dev'))
Inputs may be any that keep to these rules, and one draw needn't show every extreme that they name: `page_table`: entry p of request r is used for p < ceil(lengths[r] / 16) and is 0 otherwise. The used entries of one device's requests are distinct. Of two partners exactly one sheds: its used entries take every value from 0 to 143; the other's stay below 128. `lengths`: A device that sheds has a request of 256 tokens. `shed_slots`: for a device that sheds: distinct pages of the partner's block that no request of the partner uses. For the other device the list is not read. `expert_ids`: among the 16 requests of one device at most 2 name the same expert; the 8 experts of a request differ.
All inputs are finite; a program needn't handle non-finite values.
Results may differ from a plain program's by a relative error of at most 0.014.
Values may be sent and summed in bfloat16 or wider, within the bound.
A program may use at most 128 MiB of HBM per device.

v0:
```python
import math

import jax
import jax.numpy as jnp
from jax import lax
from jax.sharding import PartitionSpec as P

HEAD_DIMENSION = 128
KEY_VALUE_HEADS = 2
QUERY_GROUP_SIZE = 16


masked_score = -1e30
epsilon = 1e-06


def from_behind(value, axis, by):
    length = lax.axis_size(axis)
    return lax.ppermute(value, axis, [(i, (i + by) % length) for i in range(length)])


def cache_scores(source, index_table, allowed, query_head_block, scaling):
    count_of_rows = index_table.shape[0]
    collected_rows = jnp.take(source, index_table, axis=0).reshape(
        count_of_rows, -1, source.shape[-1]
    )
    key_row_width = source.shape[-1] // 2
    group_heads = query_head_block.shape[1]
    head_size = query_head_block.shape[3]
    key_entries = collected_rows[:, :, :key_row_width].reshape(
        count_of_rows, -1, group_heads, head_size
    )
    value_entries = collected_rows[:, :, key_row_width:].reshape(
        count_of_rows, -1, group_heads, head_size
    )
    scores = (
        jnp.einsum(
            "rkgd,rlkd->rkgl", query_head_block, key_entries, preferred_element_type=jnp.float32
        )
        * scaling
    )
    scores = jnp.where(allowed[:, None, None, :], scores, masked_score)
    return (scores, value_entries)


def finish_attention(score_list, value_list, query_head_block, incoming_rows, scaling):
    count_of_rows = incoming_rows.shape[0]
    key_row_width = incoming_rows.shape[-1] // 2
    group_heads = query_head_block.shape[1]
    head_size = query_head_block.shape[3]
    incoming_keys = incoming_rows[:, :key_row_width].reshape(count_of_rows, group_heads, head_size)
    incoming_values = incoming_rows[:, key_row_width:].reshape(
        count_of_rows, group_heads, head_size
    )
    fresh_score = (
        jnp.einsum(
            "rkgd,rkd->rkg", query_head_block, incoming_keys, preferred_element_type=jnp.float32
        )
        * scaling
    )
    largest = fresh_score
    for scores in score_list:
        largest = jnp.maximum(largest, jnp.max(scores, axis=-1))
    fresh_weight = jnp.exp(fresh_score - largest)
    denominator = fresh_weight
    fresh_low = lax.optimization_barrier(fresh_weight.astype(jnp.bfloat16)).astype(jnp.float32)
    summed = fresh_low[..., None] * incoming_values.astype(jnp.float32)[:, :, None, :]
    for scores, value_entries in zip(score_list, value_list):
        weights = jnp.exp(scores - largest[..., None])
        denominator = denominator + jnp.sum(weights, axis=-1)
        summed = summed + jnp.einsum(
            "rkgl,rlkd->rkgd",
            weights.astype(jnp.bfloat16),
            value_entries,
            preferred_element_type=jnp.float32,
        )
    return (summed / denominator[..., None]).reshape(count_of_rows, -1).astype(jnp.bfloat16)


def expert_block(tokens, gate_up, down_proj):
    hidden_dim = down_proj.shape[0]
    product = jnp.dot(tokens, gate_up, preferred_element_type=jnp.float32)
    hidden = (jax.nn.silu(product[:, :hidden_dim]) * product[:, hidden_dim:]).astype(jnp.bfloat16)
    return jnp.dot(hidden, down_proj, preferred_element_type=jnp.float32).astype(jnp.bfloat16)


def local(
    queries,
    new_kv,
    kv_pages,
    page_table,
    lengths,
    shed_slots,
    residual,
    norm_gain,
    expert_ids,
    gate_weights,
    w_gate_up,
    w_down,
):
    count_of_rows, model_dim = queries.shape
    pages_own, page_len, kv_width = kv_pages.shape
    table_width = page_table.shape[1]
    query_head_block = queries.reshape(
        count_of_rows, KEY_VALUE_HEADS, QUERY_GROUP_SIZE, HEAD_DIMENSION
    )
    scaling = 1.0 / math.sqrt(HEAD_DIMENSION)
    positions = jnp.arange(table_width * page_len, dtype=jnp.int32)
    allowed = positions[None, :] < lengths[:, None]
    requested = from_behind(shed_slots, "pool", 1)
    fetched = from_behind(jnp.take(kv_pages, requested, axis=0), "pool", 1)
    combined = jnp.concatenate([kv_pages, fetched], axis=0)
    scores, value_entries = cache_scores(combined, page_table, allowed, query_head_block, scaling)
    attended = finish_attention([scores], [value_entries], query_head_block, new_kv, scaling)
    merged = (residual.astype(jnp.float32) + attended.astype(jnp.float32)).astype(jnp.bfloat16)
    merged_wide = merged.astype(jnp.float32)
    normed = (
        merged_wide
        * lax.rsqrt(jnp.mean(merged_wide * merged_wide, axis=-1, keepdims=True) + epsilon)
        * norm_gain
    ).astype(jnp.bfloat16)
    top_count = expert_ids.shape[1]
    expert_count = lax.axis_size("pool") * lax.axis_size("dev")
    capacity = 2 * count_of_rows * top_count // expert_count
    flat_ids = expert_ids.reshape(-1)
    one_hot = (flat_ids[:, None] == jnp.arange(expert_count, dtype=jnp.int32)[None, :]).astype(
        jnp.int32
    )
    earlier = jnp.cumsum(one_hot, axis=0) - one_hot
    slot_rank = jnp.sum(earlier * one_hot, axis=1)
    target = flat_ids * capacity + slot_rank
    repeated = jnp.broadcast_to(normed[:, None, :], (count_of_rows, top_count, model_dim)).reshape(
        -1, model_dim
    )
    outgoing = (
        jnp.zeros((expert_count * capacity, model_dim), jnp.bfloat16).at[target].set(repeated)
    )
    gate_up = w_gate_up[0]
    down_proj = w_down[0]
    arrived = lax.all_to_all(
        outgoing.reshape(expert_count, capacity, model_dim),
        ("pool", "dev"),
        split_axis=0,
        concat_axis=0,
        tiled=True,
    )
    slot_count = arrived.shape[1]
    finished = expert_block(arrived.reshape(-1, model_dim), gate_up, down_proj).reshape(
        expert_count, slot_count, model_dim
    )
    returned = lax.all_to_all(finished, ("pool", "dev"), split_axis=0, concat_axis=0, tiled=True)
    results = returned.reshape(-1, model_dim)[target].reshape(count_of_rows, top_count, model_dim)
    expert_sum = jnp.sum(results.astype(jnp.float32) * gate_weights[:, :, None], axis=1)
    layer_out = (merged_wide + expert_sum).astype(jnp.bfloat16)
    return (attended, layer_out)


def solution(mesh):
    return jax.shard_map(
        local,
        mesh=mesh,
        in_specs=(
            P(("pool", "dev"), None),
            P(("pool", "dev"), None),
            P(("pool", "dev"), None, None),
            P(("pool", "dev"), None),
            P(("pool", "dev")),
            P(("pool", "dev")),
            P(("pool", "dev"), None),
            P(),
            P(("pool", "dev"), None),
            P(("pool", "dev"), None),
            P(("pool", "dev"), None, None),
            P(("pool", "dev"), None, None),
        ),
        out_specs=(P(("pool", "dev"), None), P(("pool", "dev"), None)),
        check_vma=False,
    )
```

profile of v0, /device:TPU:1, one launch (start us, length us, event | category | flops | bytes accessed | tf_op | source)
XLA Modules:
  0.0 141.1 jit_solution(1829059892722567815)
XLA Ops:
  0.6 4.5 %collective-permute-start = (s32[16]{0:T(128)}, s32[16]{0:T(128)S(1)}, u32[]{:S(2)}, u32[]{:S(2)}) collective-permute-start(s32[16]{0:T(128)} %param.17), channel_id=1, source_target_pairs={{0,64},{64,0},{1,65},{65,1},{2,66},{66,2},{3,67},{67,3},{4,68},{68... | collective-permute-start | bytes 200 | tf_op jit(solution)/shard_map/ppermute | solution.py:19
  5.1 0.7 compare_select_fusion
  5.8 0.7 compare_and_fusion
  6.5 0.8 copy.27
  7.3 0.7 broadcast_multiply_fusion
  8.0 0.7 iota_compare_fusion.1
  8.7 0.7 slice_convert_fusion
  10.2 2.2 %gather_fusion = bf16[16,16,512]{2,1,0:T(8,128)(2,1)S(1)} fusion(bf16[128,16,512]{2,1,0:T(8,128)(2,1)} %param.14, s32[1024]{0:T(1024)S(1)} %pad_clamp_fusion.2), kind=kCustom, calls=%fused_computation | custom fusion | bytes 524352 | tf_op jit(solution)/shard_map/jit(_take)/gather | solution.py:111
  12.9 0.9 copy.33
  14.0 7.0 %collective-permute-done.1 = bf16[16,16,512]{2,1,0:T(8,128)(2,1)S(1)} collective-permute-done((bf16[16,16,512]{2,1,0:T(8,128)(2,1)S(1)}, bf16[16,16,512]{2,1,0:T(8,128)(2,1)S(1)}, u32[]{:S(2)}, u32[]{:S(2)}) %collective-permute-start.1) | collective-permute-done | bytes 262176 | tf_op jit(solution)/shard_map/ppermute | solution.py:19
  21.0 1.8 %pad_maximum_fusion = bf16[144,16,512]{2,1,0:T(8,128)(2,1)S(1)} fusion(bf16[16,16,512]{2,1,0:T(8,128)(2,1)S(1)} %collective-permute-done.1, bf16[128,16,512]{2,1,0:T(8,128)(2,1)} %param.14), kind=kLoop, calls=%fused_computation.10 | loop fusion | flops 1179648 | bytes 4718592 | tf_op jit(solution)/shard_map/concatenate | solution.py:112
  22.8 2.7 %gather_fusion.1 = bf16[256,16,512]{2,1,0:T(8,128)(2,1)} fusion(bf16[144,16,512]{2,1,0:T(8,128)(2,1)S(1)} %pad_maximum_fusion, s32[1024]{0:T(1024)S(1)} %pad_clamp_fusion.1), kind=kCustom, calls=%fused_computation.1 | custom fusion | bytes 8389632 | tf_op jit(solution)/shard_map/jit(_take)/gather | solution.py:24
  25.6 2.6 %bitcast_select_fusion = bf16[16,256,512]{2,1,0:T(8,128)(2,1)S(1)} fusion(pred[16,256]{1,0:T(8,128)(4,1)S(1)} %broadcast_in_dim.64, bf16[16,256,512]{2,1,0:T(8,128)(2,1)} %bitcast.43), kind=kLoop, calls=%fused_computation.9 | loop fusion | flops 2097152 | bytes 8392704 | tf_op jit(solution)/shard_map/jit(_take)/select_n | solution.py:24
  28.1 2.5 %fusion.32 = (bf16[16,256,256]{2,1,0:T(8,128)(2,1)}, bf16[16,256,256]{2,1,0:T(8,128)(2,1)}) fusion(bf16[16,256,512]{2,1,0:T(8,128)(2,1)S(1)} %bitcast_select_fusion), kind=kLoop, calls=%fused_computation.62 | loop fusion | bytes 8388608 | tf_op jit(solution)/shard_map/slice | solution.py:30
  30.6 2.8 %copy.22 = bf16[16,256,256]{1,2,0:T(8,128)(2,1)S(1)} copy(bf16[16,256,256]{2,1,0:T(8,128)(2,1)} %get-tuple-element.4) | data formatting | bytes 4194304 | tf_op jit(solution)/shard_map/slice | solution.py:30
  33.5 0.5 fusion.33
  34.0 0.3 fusion.17
  34.3 2.9 %copy.24 = bf16[16,256,256]{1,2,0:T(8,128)(2,1)S(1)} copy(bf16[16,256,256]{2,1,0:T(8,128)(2,1)} %get-tuple-element.5) | data formatting | bytes 4194304 | tf_op jit(solution)/shard_map/slice | solution.py:33
  37.2 0.7 fusion.11
  38.4 2.7 %scatter_custom_fusion = bf16[256,4096]{1,0:T(8,128)(2,1)S(1)} fusion(s32[128]{0:T(128)S(1)} %fusion.28, bf16[]{:T(256)} %constant.53.clone.1, bf16[16,4096]{1,0:T(8,128)(2,1)S(1)} %fusion.23), kind=kCustom, calls=%fused_computation.19 | custom fusion | bytes 2228226 | tf_op jit(solution)/shard_map/scatter | solution.py:136
  41.1 2.7 %reshape.123 = bf16[128,2,4096]{2,1,0:T(2,128)(2,1)} reshape(bf16[256,4096]{1,0:T(8,128)(2,1)S(1)} %scatter_custom_fusion) | data formatting | bytes 4194304 | tf_op jit(solution)/shard_map/reshape | solution.py:141
  43.8 39.4 %all_to_all.10 = bf16[128,2,4096]{2,1,0:T(2,128)(2,1)S(1)} all-to-all(bf16[128,2,4096]{2,1,0:T(2,128)(2,1)} %reshape.123), channel_id=1, replica_groups=mesh['pool'=2,'dev'=64] {'pool','dev'}, dimensions={0} | all-to-all | bytes 4194304 | tf_op jit(solution)/shard_map/all_to_all | solution.py:140
  83.2 2.2 %reshape.124 = bf16[256,4096]{1,0:T(8,128)(2,1)} reshape(bf16[128,2,4096]{2,1,0:T(2,128)(2,1)S(1)} %all_to_all.10) | data formatting | bytes 4194304 | tf_op jit(solution)/shard_map/reshape | solution.py:148
  85.4 7.0 %fusion = f32[256,1536]{1,0:T(8,128)S(1)} fusion(bf16[256,4096]{1,0:T(8,128)(2,1)} %reshape.124, bf16[1,4096,1536]{2,1,0:T(8,128)(2,1)} %param.22), kind=kOutput, calls=%fused_computation.4 | convolution fusion | flops 3221225472 | bytes 16252928 | tf_op jit(solution)/shard_map/dot_general | solution.py:82
  92.5 4.6 %fusion.4 = bf16[256,4096]{1,0:T(8,128)(2,1)S(1)} fusion(bf16[1,768,4096]{2,1,0:T(8,128)(2,1)} %param.23, f32[256,1536]{1,0:T(8,128)S(1)} %fusion), kind=kOutput, calls=%fused_computation.8 | convolution fusion | flops 1612840960 | bytes 9961472 | tf_op jit(solution)/shard_map/dot_general | solution.py:84
  97.1 2.7 %reshape.125 = bf16[128,2,4096]{2,1,0:T(2,128)(2,1)} reshape(bf16[256,4096]{1,0:T(8,128)(2,1)S(1)} %fusion.4) | data formatting | bytes 4194304 | tf_op jit(solution)/shard_map/reshape | solution.py:148
  99.8 5.4 %all-to-all-start.1 = ((bf16[128,2,4096]{2,1,0:T(2,128)(2,1)}), bf16[128,2,4096]{2,1,0:T(2,128)(2,1)}, u32[]{:S(2)}, u32[]{:S(2)}) async-start(bf16[128,2,4096]{2,1,0:T(2,128)(2,1)} %reshape.125), calls=%async_computation.1 | async-start | bytes 4194304 | tf_op jit(solution)/shard_map/all_to_all | solution.py:151
  105.3 30.3 %all-to-all-done.1 = bf16[128,2,4096]{2,1,0:T(2,128)(2,1)} async-done(((bf16[128,2,4096]{2,1,0:T(2,128)(2,1)}), bf16[128,2,4096]{2,1,0:T(2,128)(2,1)}, u32[]{:S(2)}, u32[]{:S(2)}) %all-to-all-start.1) | async-done | bytes 2097184 | tf_op jit(solution)/shard_map/all_to_all | solution.py:151
  135.6 2.7 %reshape.126 = bf16[256,4096]{1,0:T(8,128)(2,1)S(1)} reshape(bf16[128,2,4096]{2,1,0:T(2,128)(2,1)} %all-to-all-done.1) | data formatting | bytes 4194304 | tf_op jit(solution)/shard_map/reshape | solution.py:152
  138.4 1.2 gather_fusion.2
  139.6 0.8 fusion.7
  140.4 0.7 fusion.24
  (36 shorter events, 2.0 us)
Async XLA Ops:
  0.6 9.6 %collective-permute-start = (s32[16]{0:T(128)}, s32[16]{0:T(128)S(1)}, u32[]{:S(2)}, u32[]{:S(2)}) collective-permute-start(s32[16]{0:T(128)} %param.17), channel_id=1, source_target_pairs={{0,64},{64,0},{1,65},{65,1},{2,66},{66,2},{3,67},{67,3},{4,68},{68... | collective-permute-start | bytes 200 | tf_op jit(solution)/shard_map/ppermute | solution.py:19
  12.5 8.5 %collective-permute-start.1 = (bf16[16,16,512]{2,1,0:T(8,128)(2,1)S(1)}, bf16[16,16,512]{2,1,0:T(8,128)(2,1)S(1)}, u32[]{:S(2)}, u32[]{:S(2)}) collective-permute-start(bf16[16,16,512]{2,1,0:T(8,128)(2,1)S(1)} %broadcast_select_fusion), channel_id=1, source_target_pairs={{0,64},{64,0},{1,65},{65,1},{2,66},{66,2},{3,67},{67,3},{4,68},{68... | collective-permute-start | bytes 786440 | tf_op jit(solution)/shard_map/ppermute | solution.py:19
  37.2 0.9 copy-start
  37.2 1.1 copy-start.2
  38.3 102.1 %copy-start.1 = (bf16[16,4096]{1,0:T(8,128)(2,1)}, bf16[16,4096]{1,0:T(8,128)(2,1)S(1)}, u32[]{:S(2)}) copy-start(bf16[16,4096]{1,0:T(8,128)(2,1)S(1)} %get-tuple-element.3) | copy-start | bytes 393220
  99.8 5.4 %copy-start.3 = (f32[16,8]{0,1:T(8,128)S(1)}, f32[16,8]{0,1:T(8,128)}, u32[]{:S(2)}) copy-start(f32[16,8]{0,1:T(8,128)} %param.21) | copy-start | bytes 1540
  99.8 35.8 %all-to-all-start.1 = ((bf16[128,2,4096]{2,1,0:T(2,128)(2,1)}), bf16[128,2,4096]{2,1,0:T(2,128)(2,1)}, u32[]{:S(2)}, u32[]{:S(2)}) async-start(bf16[128,2,4096]{2,1,0:T(2,128)(2,1)} %reshape.125), calls=%async_computation.1 | async-start | bytes 4194304 | tf_op jit(solution)/shard_map/all_to_all | solution.py:151
where the time goes:
time: 142 us; the launch traced here: 141 us
  blocking collectives  39.4 us (28%)
  waiting for transfers between devices  37.4 us (26%)
  local copies, waits for them, and re-layouts  29.8 us (21%)
  matrix products  13 us (9%)
  other arithmetic  10.6 us (7%)
  starting transfers between devices  9.96 us (7%)
    all_to_all x1, blocking collectives, local(): lax.all_to_all(outgoing.reshape(expert_count, capacity, model_dim), ('poo...  39.4 us
    all_to_all x1, waiting for transfers between devices, local(): lax.all_to_all(finished, ('pool', 'dev'), split_axis=0, concat_axis=0, ti...  30.3 us
    ppermute x2, waiting for transfers between devices, from_behind(): lax.ppermute(value, axis, [(i, (i + by) % length) for i in range(length)])  7.02 us
    dot_general x1, matrix products, expert_block(): product = jnp.dot(tokens, gate_up, preferred_element_type=jnp.float32)  7.02 us
    all_to_all x1, starting transfers between devices, local(): lax.all_to_all(finished, ('pool', 'dev'), split_axis=0, concat_axis=0, ti...  5.37 us
    slice x2, local copies, waits for them, and re-layouts, cache_scores(): collected_rows[:, :, :key_row_width]  5.3 us
    dot_general x1, matrix products, expert_block(): jnp.dot(hidden, down_proj, preferred_element_type=jnp.float32)  4.65 us
    ppermute x2, starting transfers between devices, from_behind(): lax.ppermute(value, axis, [(i, (i + by) % length) for i in range(length)])  4.59 us
  transfers between devices with their start and end apart: 3, of which 2 were waited for; matrix products, arithmetic and copies ran while one was open for 5% of the time, Pallas kernels for 0%

commit v1 on v0

--- a/solution.py
+++ b/solution.py
@@ -3,6 +3,8 @@
 import jax
 import jax.numpy as jnp
 from jax import lax
+from jax.experimental import pallas as pl
+from jax.experimental.pallas import tpu as pltpu
 from jax.sharding import PartitionSpec as P
 
 HEAD_DIMENSION = 128
@@ -77,11 +79,322 @@
     return (summed / denominator[..., None]).reshape(count_of_rows, -1).astype(jnp.bfloat16)
 
 
-def expert_block(tokens, gate_up, down_proj):
-    hidden_dim = down_proj.shape[0]
-    product = jnp.dot(tokens, gate_up, preferred_element_type=jnp.float32)
-    hidden = (jax.nn.silu(product[:, :hidden_dim]) * product[:, hidden_dim:]).astype(jnp.bfloat16)
-    return jnp.dot(hidden, down_proj, preferred_element_type=jnp.float32).astype(jnp.bfloat16)
+MESH_ID = pl.DeviceIdType.MESH
+ROTATIONS = ((0, 1, 2), (1, 2, 0), (2, 0, 1))
+SIDE = 4
+PEERS = 8
+CHUNKS = ((0, 0, 6), (1, 6, 5), (2, 11, 5), (0, 16, 5), (1, 21, 6), (2, 27, 5))
+
+
+def coordinates():
+    pool = lax.axis_index("pool")
+    dev = lax.axis_index("dev")
+    x = lax.div(dev, 16)
+    y = lax.rem(lax.div(dev, 2), 4)
+    z = pool * 2 + lax.rem(lax.div(dev, 8), 2)
+    return (x, y, z), lax.rem(dev, 2)
+
+
+def device_at(place, core):
+    x, y, z = place
+    return (lax.div(z, 2), x * 16 + lax.rem(z, 2) * 8 + y * 2 + core)
+
+
+def shifted(place, axis, by):
+    return tuple(
+        lax.rem(value + by + SIDE, SIDE) if i == axis else value for i, value in enumerate(place)
+    )
+
+
+def routed_experts_kernel(
+    normed, codes, merged, gate_up_hbm, down_hbm, out,
+    gate_up, down, gathered, select, weight, first, packed, second, third, product, hidden,
+    sent_back, back_one, back_two, partial, own_sum, back_three,
+    w_sems, code_s, code_r, s1_s, s1_r, s2_s, s2_r, s3_s, s3_r, r3_s, r3_r, r2_s, r2_r, r1_s, r1_r,
+):
+    place, core = coordinates()
+    hidden_dim = down.shape[0]
+    loads = [
+        pltpu.make_async_copy(gate_up_hbm, gate_up, w_sems.at[0]),
+        pltpu.make_async_copy(down_hbm, down, w_sems.at[1]),
+    ]
+    for load in loads:
+        load.start()
+
+    def other(axis, by, flip):
+        return device_at(shifted(place, axis, by), lax.rem(core + flip, 2))
+
+    barrier = pltpu.get_barrier_semaphore()
+    neighbours = [other(0, 0, 1)] + [
+        other(axis, by, flip) for axis in range(3) for by in (1, 2, 3) for flip in (0, 1)
+    ]
+    for neighbour in neighbours:
+        pl.semaphore_signal(barrier, inc=1, device_id=neighbour, device_id_type=MESH_ID)
+    pl.semaphore_wait(barrier, len(neighbours))
+
+    sends = []
+
+    def send(source, target, send_sem, recv_sem, device):
+        copy = pltpu.make_async_remote_copy(
+            src_ref=source, dst_ref=target, send_sem=send_sem, recv_sem=recv_sem,
+            device_id=device, device_id_type=MESH_ID,
+        )
+        copy.start()
+        sends.append(copy)
+        return copy
+
+    def columns(start, count):
+        return pl.ds(start * 128, count * 128)
+
+    code_copies = []
+    for i, (axis, by, flip) in enumerate(
+        [(0, 0, 1)] + [(a, b, f) for a in range(3) for b in (1, 2, 3) for f in (0, 1)]
+    ):
+        code_copies.append(
+            send(codes, gathered.at[i], code_s.at[i], code_r.at[i], other(axis, by, flip))
+        )
+    first_copies = []
+    for c, (r, start, count) in enumerate(CHUNKS):
+        axis = ROTATIONS[r][0]
+        copies = []
+        for s in range(1, PEERS):
+            copies.append(
+                send(
+                    normed.at[:, columns(start, count)],
+                    first.at[s, :, columns(start, count)],
+                    s1_s.at[c, s], s1_r.at[c, s],
+                    other(axis, s // 2, s % 2),
+                )
+            )
+        first_copies.append(copies)
+    first[0] = normed[...]
+    for copy in code_copies:
+        copy.wait_recv()
+
+    row = lax.broadcasted_iota(jnp.int32, (256, 1), 0)
+    lane = lax.broadcasted_iota(jnp.int32, (1, 128), 1)
+    slot = lax.rem(row, 2)
+    row_peer = lax.rem(lax.div(row, 2), PEERS)
+    same_peer = row_peer == lax.div(lane, 16)
+    lane_peer = lax.div(lax.broadcasted_iota(jnp.int32, (16, 128), 1), 16)
+    for r, (a0, a1, a2) in enumerate(ROTATIONS):
+        entries = jnp.where(lane_peer == 0, codes[...], 0.0)
+        entries = jnp.where(lane_peer == 1, gathered[0], entries)
+        for s in range(2, PEERS):
+            entries = jnp.where(lane_peer == s, gathered[1 + a0 * 6 + s - 2], entries)
+        where = list(place)
+        where[a1] = lax.rem(place[a1] + lax.div(row, 64), SIDE)
+        where[a2] = lax.rem(place[a2] + lax.rem(lax.div(row, 16), SIDE), SIDE)
+        x, y, z = where
+        expert = lax.div(z, 2) * 64 + x * 16 + lax.rem(z, 2) * 8 + y * 2 + core
+        wanted = (expert * 2 + slot).astype(jnp.float32)
+        chosen = jnp.zeros((256, 128), jnp.float32)
+        gates = jnp.zeros((256, 128), jnp.float32)
+        for k in range(8):
+            match = same_peer & (entries[k : k + 1, :] == wanted)
+            chosen = jnp.where(match, 1.0, chosen)
+            gates = jnp.where(match, entries[8 + k : 9 + k, :], gates)
+        select[r] = chosen.astype(jnp.bfloat16)
+        for part in range(3):
+            piece = gates.astype(jnp.bfloat16)
+            weight[r, part] = piece
+            gates = gates - piece.astype(jnp.float32)
+
+    second_copies = []
+    for c, (r, start, count) in enumerate(CHUNKS):
+        a1 = ROTATIONS[r][1]
+        for copy in first_copies[c]:
+            copy.wait_recv()
+        cols = columns(start, count)
+        rows = first[:, :, cols].reshape(PEERS * 16, count * 128)
+        block = jnp.dot(select[r], rows, preferred_element_type=jnp.float32).astype(jnp.bfloat16)
+        block = block.reshape(SIDE, SIDE, 16, count * 128)
+        second[0, :, :, cols] = block[0]
+        copies = []
+        for d in (2, 1, 3):
+            packed[d, :, :, cols] = block[d]
+        for d in (2, 1, 3):
+            copies.append(
+                send(
+                    packed.at[d, :, :, cols], second.at[d, :, :, cols],
+                    s2_s.at[c, d], s2_r.at[c, d], other(a1, d, 0),
+                )
+            )
+        second_copies.append(copies)
+    third_copies = []
+    for c, (r, start, count) in enumerate(CHUNKS):
+        a2 = ROTATIONS[r][2]
+        for copy in second_copies[c]:
+            copy.wait_recv()
+        cols = columns(start, count)
+        copies = []
+        for d in (2, 1, 3):
+            copies.append(
+                send(
+                    second.at[:, d, :, cols], third.at[d, :, :, cols],
+                    s3_s.at[c, d], s3_r.at[c, d], other(a2, d, 0),
+                )
+            )
+        third[0, :, :, cols] = second[:, 0, :, cols]
+        third_copies.append(copies)
+
+    canon = lax.broadcasted_iota(jnp.int32, (256, 256), 0)
+    local = lax.broadcasted_iota(jnp.int32, (256, 256), 1)
+    apart = (
+        lax.rem(lax.div(canon, 4), SIDE),
+        lax.rem(lax.div(canon, 16), SIDE),
+        lax.div(canon, 64),
+    )
+    orders = []
+    for a0, a1, a2 in ROTATIONS:
+        index = apart[a2] * 64 + apart[a1] * 16 + apart[a0] * 4 + lax.rem(canon, 4)
+        orders.append((index == local).astype(jnp.bfloat16))
+
+    loads[0].wait()
+    for c, (r, start, count) in enumerate(CHUNKS):
+        for copy in third_copies[c]:
+            copy.wait_recv()
+        cols = columns(start, count)
+        tokens = third[:, :, :, cols].reshape(256, count * 128)
+        if r:
+            tokens = jnp.dot(orders[r], tokens, preferred_element_type=jnp.float32)
+            tokens = tokens.astype(jnp.bfloat16)
+        for n in range(0, 2 * hidden_dim, 512):
+            piece = jnp.dot(
+                tokens, gate_up[pl.ds(start * 128, count * 128), pl.ds(n, 512)],
+                preferred_element_type=jnp.float32,
+            )
+            if c:
+                piece = product[:, pl.ds(n, 512)] + piece
+            product[:, pl.ds(n, 512)] = piece
+    gate = product[:, :hidden_dim]
+    active = (gate / (1.0 + jnp.exp(-gate)) * product[:, hidden_dim:]).astype(jnp.bfloat16)
+    hidden[0] = active
+    for r in (1, 2):
+        turned = lax.dot_general(
+            orders[r], active, (((0,), (0,)), ((), ())), preferred_element_type=jnp.float32
+        )
+        hidden[r] = turned.astype(jnp.bfloat16)
+
+    loads[1].wait()
+    one_copies = []
+    for c, (r, start, count) in enumerate(CHUNKS):
+        a2 = ROTATIONS[r][2]
+        cols = columns(start, count)
+        finished = jnp.dot(hidden[r], down[:, cols], preferred_element_type=jnp.float32)
+        finished = finished.astype(jnp.bfloat16).reshape(SIDE, SIDE, 16, count * 128)
+        back_one[0, :, :, cols] = finished[0]
+        for d in (2, 1, 3):
+            sent_back[d, :, :, cols] = finished[d]
+        copies = []
+        for d in (2, 1, 3):
+            copies.append(
+                send(
+                    sent_back.at[d, :, :, cols], back_one.at[d, :, :, cols],
+                    r3_s.at[c, d], r3_r.at[c, d], other(a2, -d, 0),
+                )
+            )
+        one_copies.append(copies)
+    two_copies = []
+    for c, (r, start, count) in enumerate(CHUNKS):
+        a1 = ROTATIONS[r][1]
+        for copy in one_copies[c]:
+            copy.wait_recv()
+        cols = columns(start, count)
+        copies = []
+        for d in (2, 1, 3):
+            copies.append(
+                send(
+                    back_one.at[:, d, :, cols], back_two.at[d, :, :, cols],
+                    r2_s.at[c, d], r2_r.at[c, d], other(a1, -d, 0),
+                )
+            )
+        back_two[0, :, :, cols] = back_one[:, 0, :, cols]
+        two_copies.append(copies)
+    three_copies = []
+    for c, (r, start, count) in enumerate(CHUNKS):
+        a0 = ROTATIONS[r][0]
+        for copy in two_copies[c]:
+            copy.wait_recv()
+        cols = columns(start, count)
+        results = back_two[:, :, :, cols].reshape(256, count * 128)
+        total = None
+        for part in range(3):
+            piece = lax.dot_general(
+                weight[r, part], results, (((0,), (0,)), ((), ())),
+                preferred_element_type=jnp.float32,
+            )
+            total = piece if total is None else total + piece
+        total = total.reshape(PEERS, 16, count * 128)
+        own_sum[:, cols] = total[0]
+        partial[1:, :, cols] = total[1:].astype(jnp.bfloat16)
+        copies = []
+        for s in range(1, PEERS):
+            copies.append(
+                send(
+                    partial.at[s, :, cols], back_three.at[s, :, cols],
+                    r1_s.at[c, s], r1_r.at[c, s], other(a0, -(s // 2), s % 2),
+                )
+            )
+        three_copies.append(copies)
+    for c, (r, start, count) in enumerate(CHUNKS):
+        for copy in three_copies[c]:
+            copy.wait_recv()
+        cols = columns(start, count)
+        total = own_sum[:, cols]
+        for s in range(1, PEERS):
+            total = total + back_three[s, :, cols].astype(jnp.float32)
+        out[:, cols] = (merged[:, cols].astype(jnp.float32) + total).astype(jnp.bfloat16)
+    for copy in sends:
+        copy.wait_send()
+
+
+def routed_experts(normed, codes, merged, gate_up, down):
+    width = normed.shape[1]
+    hidden_dim = down.shape[0]
+    chunks = len(CHUNKS)
+    bf16, f32 = jnp.bfloat16, jnp.float32
+    vmem = pl.BlockSpec(memory_space=pltpu.VMEM)
+    hbm = pl.BlockSpec(memory_space=pl.ANY)
+    block = pltpu.VMEM((SIDE, SIDE, 16, width), bf16)
+    peers = pltpu.VMEM((PEERS, 16, width), bf16)
+    dma = pltpu.SemaphoreType.DMA
+    return pl.pallas_call(
+        routed_experts_kernel,
+        out_shape=jax.ShapeDtypeStruct(normed.shape, bf16),
+        in_specs=[vmem, vmem, vmem, hbm, hbm],
+        out_specs=vmem,
+        scratch_shapes=[
+            pltpu.VMEM(gate_up.shape, bf16),
+            pltpu.VMEM(down.shape, bf16),
+            pltpu.VMEM((19, 16, 128), f32),
+            pltpu.VMEM((3, 256, 128), bf16),
+            pltpu.VMEM((3, 3, 256, 128), bf16),
+            peers,
+            block,
+            block,
+            block,
+            pltpu.VMEM((256, 2 * hidden_dim), f32),
+            pltpu.VMEM((3, 256, hidden_dim), bf16),
+            block,
+            block,
+            block,
+            peers,
+            pltpu.VMEM((16, width), f32),
+            peers,
+            dma((2,)),
+            dma((19,)), dma((19,)),
+            dma((chunks, PEERS)), dma((chunks, PEERS)),
+            dma((chunks, SIDE)), dma((chunks, SIDE)),
+            dma((chunks, SIDE)), dma((chunks, SIDE)),
+            dma((chunks, SIDE)), dma((chunks, SIDE)),
+            dma((chunks, SIDE)), dma((chunks, SIDE)),
+            dma((chunks, PEERS)), dma((chunks, PEERS)),
+        ],
+        compiler_params=pltpu.CompilerParams(
+            collective_id=0, has_side_effects=True, vmem_limit_bytes=60 * 1024 * 1024
+        ),
+    )(normed, codes, merged, gate_up, down)
 
 
 def local(
@@ -119,39 +432,15 @@
         * lax.rsqrt(jnp.mean(merged_wide * merged_wide, axis=-1, keepdims=True) + epsilon)
         * norm_gain
     ).astype(jnp.bfloat16)
-    top_count = expert_ids.shape[1]
-    expert_count = lax.axis_size("pool") * lax.axis_size("dev")
-    capacity = 2 * count_of_rows * top_count // expert_count
-    flat_ids = expert_ids.reshape(-1)
-    one_hot = (flat_ids[:, None] == jnp.arange(expert_count, dtype=jnp.int32)[None, :]).astype(
-        jnp.int32
-    )
-    earlier = jnp.cumsum(one_hot, axis=0) - one_hot
-    slot_rank = jnp.sum(earlier * one_hot, axis=1)
-    target = flat_ids * capacity + slot_rank
-    repeated = jnp.broadcast_to(normed[:, None, :], (count_of_rows, top_count, model_dim)).reshape(
-        -1, model_dim
-    )
-    outgoing = (
-        jnp.zeros((expert_count * capacity, model_dim), jnp.bfloat16).at[target].set(repeated)
-    )
-    gate_up = w_gate_up[0]
-    down_proj = w_down[0]
-    arrived = lax.all_to_all(
-        outgoing.reshape(expert_count, capacity, model_dim),
-        ("pool", "dev"),
-        split_axis=0,
-        concat_axis=0,
-        tiled=True,
-    )
-    slot_count = arrived.shape[1]
-    finished = expert_block(arrived.reshape(-1, model_dim), gate_up, down_proj).reshape(
-        expert_count, slot_count, model_dim
-    )
-    returned = lax.all_to_all(finished, ("pool", "dev"), split_axis=0, concat_axis=0, tiled=True)
-    results = returned.reshape(-1, model_dim)[target].reshape(count_of_rows, top_count, model_dim)
-    expert_sum = jnp.sum(results.astype(jnp.float32) * gate_weights[:, :, None], axis=1)
-    layer_out = (merged_wide + expert_sum).astype(jnp.bfloat16)
+    same = expert_ids[:, :, None, None] == expert_ids[None, None, :, :]
+    row_index = jnp.arange(count_of_rows, dtype=jnp.int32)
+    before = row_index[:, None, None, None] > row_index[None, None, :, None]
+    slot_rank = jnp.sum((same & before).astype(jnp.int32), axis=(2, 3))
+    codes = jnp.concatenate(
+        [(expert_ids * 2 + slot_rank).astype(jnp.float32).T, gate_weights.T], axis=0
+    )
+    codes = jnp.tile(codes, (1, PEERS))
+    layer_out = routed_experts(normed, codes, merged, w_gate_up[0], w_down[0])
     return (attended, layer_out)
 
 

time: 142 us -> 109 us (0.77)
  Pallas kernels: 0 us -> 64 us
  blocking collectives: 39.4 us -> 0 us
  waiting for transfers between devices: 37.4 us -> 6.27 us
  matrix products: 13 us -> 1.36 us
  local copies, waits for them, and re-layouts: 29.8 us -> 18.5 us
  starting transfers between devices: 9.96 us -> 4.59 us
  other arithmetic: 10.6 us -> 12.6 us
    pallas_call x0 -> x1, Pallas kernels: none -> 64 us  [routed_experts(): pl.pallas_call(routed_experts_kernel, out_shape=jax.ShapeDtypeStruct(norm...]
    all_to_all x1 -> x0, blocking collectives: 39.4 us -> none  [local(): lax.all_to_all(outgoing.reshape(expert_count, capacity, model_dim), ('poo...]
    all_to_all x1 -> x0, waiting for transfers between devices: 30.3 us -> none  [local(): lax.all_to_all(finished, ('pool', 'dev'), split_axis=0, concat_axis=0, ti...]
    dot_general x2 -> x0, matrix products: 11.7 us -> none  [the longest x1 7.02 us: expert_block(): product = jnp.dot(tokens, gate_up, preferred_element_type=jnp.float32)]
    reshape x4 -> x0, local copies, waits for them, and re-layouts: 10.3 us -> none  [the longest x1 2.74 us: local(): returned.reshape(-1, model_dim)[target]]
    all_to_all x1 -> x0, starting transfers between devices: 5.37 us -> none  [local(): lax.all_to_all(finished, ('pool', 'dev'), split_axis=0, concat_axis=0, ti...]
    scatter x1 -> x0, local copies, waits for them, and re-layouts: 2.73 us -> none  [local(): jnp.zeros((expert_count * capacity, model_dim), jnp.bfloat16).at[target]]
    reduce_sum x2 -> x1, other arithmetic: 0.96 us -> 3.22 us  [local(): slot_rank = jnp.sum((same & before).astype(jnp.int32), axis=(2, 3))]
  transfers between devices with their start and end apart: 3 -> 2, of which waited for: 2 -> 1; matrix products, arithmetic and copies ran while one was open for 5% -> 9% of each run, Pallas kernels for 0% -> 0%
where the time goes in v1:
time: 109 us; the launch traced here: 108 us
  Pallas kernels  64 us (59%)
  local copies, waits for them, and re-layouts  18.5 us (17%)
  other arithmetic  12.6 us (12%)
  waiting for transfers between devices  6.27 us (6%)
  starting transfers between devices  4.59 us (4%)
  matrix products  1.36 us (1%)
    pallas_call x1, Pallas kernels, routed_experts(): pl.pallas_call(routed_experts_kernel, out_shape=jax.ShapeDtypeStruct(norm...  64 us
    ppermute x2, waiting for transfers between devices, from_behind(): lax.ppermute(value, axis, [(i, (i + by) % length) for i in range(length)])  6.27 us
    slice x2, local copies, waits for them, and re-layouts, cache_scores(): collected_rows[:, :, :key_row_width]  5.3 us
    ppermute x2, starting transfers between devices, from_behind(): lax.ppermute(value, axis, [(i, (i + by) % length) for i in range(length)])  4.59 us
    unnamed x10, local copies, waits for them, and re-layouts  4.2 us
    select_n x2, other arithmetic, cache_scores(): jnp.take(source, index_table, axis=0)  3.28 us
    reduce_sum x1, other arithmetic, local(): slot_rank = jnp.sum((same & before).astype(jnp.int32), axis=(2, 3))  3.22 us
    slice x1, local copies, waits for them, and re-layouts, cache_scores(): collected_rows[:, :, key_row_width:]  3.04 us
  transfers between devices with their start and end apart: 2, of which 1 were waited for; matrix products, arithmetic and copies ran while one was open for 9% of the time, Pallas kernels for 0%

profile of v1, /device:TPU:1, one launch (start us, length us, event | category | flops | bytes accessed | tf_op | source)
XLA Modules:
  0.0 108.1 jit_solution(2963089561685667741)
XLA Ops:
  0.6 4.5 %collective-permute-start = (s32[16]{0:T(128)}, s32[16]{0:T(128)S(1)}, u32[]{:S(2)}, u32[]{:S(2)}) collective-permute-start(s32[16]{0:T(128)} %param.17), channel_id=1, source_target_pairs={{0,64},{64,0},{1,65},{65,1},{2,66},{66,2},{3,67},{67,3},{4,68},{68... | collective-permute-start | bytes 200 | tf_op jit(solution)/shard_map/ppermute | solution.py:21
  5.1 0.7 compare_select_fusion
  5.8 0.7 compare_and_fusion
  6.5 0.7 iota_compare_fusion
  7.3 0.7 slice_convert_fusion
  8.0 0.8 copy.30
  8.7 3.2 %convert_reduce_fusion = s32[16,8]{1,0:T(8,128)S(1)} fusion(s32[16,8]{0,1:T(8,128)} %param.20, s32[16,8]{1,0:T(8,128)S(1)} %copy.30, pred[16,16]{1,0:T(8,128)(4,1)S(1)} %iota_compare_fusion.1), kind=kLoop, calls=%fused_computation.10 | loop fusion | flops 65408 | bytes 1792 | tf_op jit(solution)/shard_map/reduce_sum | solution.py:438
  12.0 0.8 copy.32
  12.8 0.1 reshape.104
  12.9 2.2 %gather_fusion = bf16[16,16,512]{2,1,0:T(8,128)(2,1)S(1)} fusion(bf16[128,16,512]{2,1,0:T(8,128)(2,1)} %param.14, s32[1024]{0:T(1024)S(1)} %pad_clamp_fusion.1), kind=kCustom, calls=%fused_computation | custom fusion | bytes 524352 | tf_op jit(solution)/shard_map/jit(_take)/gather | solution.py:424
  15.1 0.1 broadcast_select_fusion
  15.2 0.1 collective-permute-start.1
  15.3 0.1 broadcast_in_dim.54
  15.4 0.1 broadcast_in_dim.55
  15.5 0.9 copy.38
  16.6 0.7 tile.10.codes
  17.3 0.2 fusion.15
  17.4 6.3 %collective-permute-done.1 = bf16[16,16,512]{2,1,0:T(8,128)(2,1)S(1)} collective-permute-done((bf16[16,16,512]{2,1,0:T(8,128)(2,1)S(1)}, bf16[16,16,512]{2,1,0:T(8,128)(2,1)S(1)}, u32[]{:S(2)}, u32[]{:S(2)}) %collective-permute-start.1) | collective-permute-done | bytes 262176 | tf_op jit(solution)/shard_map/ppermute | solution.py:21
  23.7 1.8 %pad_maximum_fusion = bf16[144,16,512]{2,1,0:T(8,128)(2,1)S(1)} fusion(bf16[16,16,512]{2,1,0:T(8,128)(2,1)S(1)} %collective-permute-done.1, bf16[128,16,512]{2,1,0:T(8,128)(2,1)} %param.14), kind=kLoop, calls=%fused_computation.3 | loop fusion | flops 1179648 | bytes 4718592 | tf_op jit(solution)/shard_map/concatenate | solution.py:425
  25.5 2.7 %gather_fusion.1 = bf16[256,16,512]{2,1,0:T(8,128)(2,1)} fusion(bf16[144,16,512]{2,1,0:T(8,128)(2,1)S(1)} %pad_maximum_fusion, s32[1024]{0:T(1024)S(1)} %pad_clamp_fusion), kind=kCustom, calls=%fused_computation.1 | custom fusion | bytes 8389632 | tf_op jit(solution)/shard_map/jit(_take)/gather | solution.py:26
  28.2 2.6 %bitcast_select_fusion = bf16[16,256,512]{2,1,0:T(8,128)(2,1)S(1)} fusion(pred[16,256]{1,0:T(8,128)(4,1)S(1)} %broadcast_in_dim.55, bf16[16,256,512]{2,1,0:T(8,128)(2,1)} %bitcast.27), kind=kLoop, calls=%fused_computation.2 | loop fusion | flops 2097152 | bytes 8392704 | tf_op jit(solution)/shard_map/jit(_take)/select_n | solution.py:26
  30.8 2.5 %fusion.13 = (bf16[16,256,256]{2,1,0:T(8,128)(2,1)}, bf16[16,256,256]{2,1,0:T(8,128)(2,1)}) fusion(bf16[16,256,512]{2,1,0:T(8,128)(2,1)S(1)} %bitcast_select_fusion), kind=kLoop, calls=%fused_computation.39 | loop fusion | bytes 8388608 | tf_op jit(solution)/shard_map/slice | solution.py:32
  33.3 2.8 %copy.26 = bf16[16,256,256]{1,2,0:T(8,128)(2,1)S(1)} copy(bf16[16,256,256]{2,1,0:T(8,128)(2,1)} %get-tuple-element.5) | data formatting | bytes 4194304 | tf_op jit(solution)/shard_map/slice | solution.py:32
  36.1 0.5 fusion.14
  36.7 0.3 fusion.4
  37.0 3.0 %copy.28 = bf16[16,256,256]{1,2,0:T(8,128)(2,1)S(1)} copy(bf16[16,256,256]{2,1,0:T(8,128)(2,1)} %get-tuple-element.6) | data formatting | bytes 4194304 | tf_op jit(solution)/shard_map/slice | solution.py:35
  40.1 0.7 fusion.3
  40.8 0.2 copy-done.1
  40.9 0.8 fusion.6
  41.8 0.8 fusion.8.normed
  42.6 64.0 %shard_map.131 = bf16[16,4096]{1,0:T(8,128)(2,1)} custom-call(bf16[16,4096]{1,0:T(8,128)(2,1)} %fusion.8.normed, f32[16,128]{1,0:T(8,128)} %tile.10.codes, bf16[16,4096]{1,0:T(8,128)(2,1)} %copy-done, bf16[4096,1536]{1,0:T(8,128)(2,1)} %bitcast.28, bf16[768,4096]{1,0:T(8,128)(2,1)} %bitcast.30), custom_call_target="tpu_custom_call" | custom-call | tf_op jit(solution)/shard_map/pallas_call | solution.py:362
  106.6 1.6 %copy.43 = bf16[16,4096]{1,0:T(8,128)(2,1)} copy(bf16[16,4096]{1,0:T(8,128)(2,1)} %shard_map.131) | data formatting | bytes 262144
  (21 shorter events, 0.3 us)
Async XLA Ops:
  0.6 12.3 %collective-permute-start = (s32[16]{0:T(128)}, s32[16]{0:T(128)S(1)}, u32[]{:S(2)}, u32[]{:S(2)}) collective-permute-start(s32[16]{0:T(128)} %param.17), channel_id=1, source_target_pairs={{0,64},{64,0},{1,65},{65,1},{2,66},{66,2},{3,67},{67,3},{4,68},{68... | collective-permute-start | bytes 200 | tf_op jit(solution)/shard_map/ppermute | solution.py:21
  15.2 8.5 %collective-permute-start.1 = (bf16[16,16,512]{2,1,0:T(8,128)(2,1)S(1)}, bf16[16,16,512]{2,1,0:T(8,128)(2,1)S(1)}, u32[]{:S(2)}, u32[]{:S(2)}) collective-permute-start(bf16[16,16,512]{2,1,0:T(8,128)(2,1)S(1)} %broadcast_select_fusion), channel_id=1, source_target_pairs={{0,64},{64,0},{1,65},{65,1},{2,66},{66,2},{3,67},{67,3},{4,68},{68... | collective-permute-start | bytes 786440 | tf_op jit(solution)/shard_map/ppermute | solution.py:21
  40.0 0.9 copy-start.1
  40.1 1.7 %copy-start.2 = (f32[4096]{0:T(1024)S(1)}, f32[4096]{0:T(1024)}, u32[]{:S(2)}) copy-start(f32[4096]{0:T(1024)} %param.19) | copy-start | bytes 49156
  41.8 0.8 copy-start

commit v2 on v1

--- a/solution.py
+++ b/solution.py
@@ -7,77 +7,17 @@
 from jax.experimental.pallas import tpu as pltpu
 from jax.sharding import PartitionSpec as P
 
-HEAD_DIMENSION = 128
-KEY_VALUE_HEADS = 2
-QUERY_GROUP_SIZE = 16
-
+HEAD = 128
+GROUPS = 2
+GROUP_HEADS = 16
+ROWS = 16
+PAGE = 16
+TILE_PAGES = 16
+TILE = TILE_PAGES * PAGE
+EXTRA = 128
 
 masked_score = -1e30
 epsilon = 1e-06
-
-
-def from_behind(value, axis, by):
-    length = lax.axis_size(axis)
-    return lax.ppermute(value, axis, [(i, (i + by) % length) for i in range(length)])
-
-
-def cache_scores(source, index_table, allowed, query_head_block, scaling):
-    count_of_rows = index_table.shape[0]
-    collected_rows = jnp.take(source, index_table, axis=0).reshape(
-        count_of_rows, -1, source.shape[-1]
-    )
-    key_row_width = source.shape[-1] // 2
-    group_heads = query_head_block.shape[1]
-    head_size = query_head_block.shape[3]
-    key_entries = collected_rows[:, :, :key_row_width].reshape(
-        count_of_rows, -1, group_heads, head_size
-    )
-    value_entries = collected_rows[:, :, key_row_width:].reshape(
-        count_of_rows, -1, group_heads, head_size
-    )
-    scores = (
-        jnp.einsum(
-            "rkgd,rlkd->rkgl", query_head_block, key_entries, preferred_element_type=jnp.float32
-        )
-        * scaling
-    )
-    scores = jnp.where(allowed[:, None, None, :], scores, masked_score)
-    return (scores, value_entries)
-
-
-def finish_attention(score_list, value_list, query_head_block, incoming_rows, scaling):
-    count_of_rows = incoming_rows.shape[0]
-    key_row_width = incoming_rows.shape[-1] // 2
-    group_heads = query_head_block.shape[1]
-    head_size = query_head_block.shape[3]
-    incoming_keys = incoming_rows[:, :key_row_width].reshape(count_of_rows, group_heads, head_size)
-    incoming_values = incoming_rows[:, key_row_width:].reshape(
-        count_of_rows, group_heads, head_size
-    )
-    fresh_score = (
-        jnp.einsum(
-            "rkgd,rkd->rkg", query_head_block, incoming_keys, preferred_element_type=jnp.float32
-        )
-        * scaling
-    )
-    largest = fresh_score
-    for scores in score_list:
-        largest = jnp.maximum(largest, jnp.max(scores, axis=-1))
-    fresh_weight = jnp.exp(fresh_score - largest)
-    denominator = fresh_weight
-    fresh_low = lax.optimization_barrier(fresh_weight.astype(jnp.bfloat16)).astype(jnp.float32)
-    summed = fresh_low[..., None] * incoming_values.astype(jnp.float32)[:, :, None, :]
-    for scores, value_entries in zip(score_list, value_list):
-        weights = jnp.exp(scores - largest[..., None])
-        denominator = denominator + jnp.sum(weights, axis=-1)
-        summed = summed + jnp.einsum(
-            "rkgl,rlkd->rkgd",
-            weights.astype(jnp.bfloat16),
-            value_entries,
-            preferred_element_type=jnp.float32,
-        )
-    return (summed / denominator[..., None]).reshape(count_of_rows, -1).astype(jnp.bfloat16)
-
 
 MESH_ID = pl.DeviceIdType.MESH
 ROTATIONS = ((0, 1, 2), (1, 2, 0), (2, 0, 1))
@@ -106,20 +46,22 @@
     )
 
 
-def routed_experts_kernel(
-    normed, codes, merged, gate_up_hbm, down_hbm, out,
+def layer_kernel(
+    queries, new_kv, pages_hbm, page_table, lengths, shed_list, residual, gain, ids, gate_in,
+    gate_up_hbm, down_hbm, attended, merged, expert_sum,
+    pages, extra, wanted_list, wanted_scalar, shed_out, shed_in, heads, scores, extra_scores,
+    peak, weight_sum, summed, normed, codes,
     gate_up, down, gathered, select, weight, first, packed, second, third, product, hidden,
-    sent_back, back_one, back_two, partial, own_sum, back_three,
-    w_sems, code_s, code_r, s1_s, s1_r, s2_s, s2_r, s3_s, s3_r, r3_s, r3_r, r2_s, r2_r, r1_s, r1_r,
+    sent_back, back_one, back_two, partial, back_three,
+    w_sems, shed_sems, code_s, code_r, s1_s, s1_r, s2_s, s2_r, s3_s, s3_r,
+    r3_s, r3_r, r2_s, r2_r, r1_s, r1_r,
 ):
+    bf16, f32 = jnp.bfloat16, jnp.float32
     place, core = coordinates()
     hidden_dim = down.shape[0]
-    loads = [
-        pltpu.make_async_copy(gate_up_hbm, gate_up, w_sems.at[0]),
-        pltpu.make_async_copy(down_hbm, down, w_sems.at[1]),
-    ]
-    for load in loads:
-        load.start()
+    own_pages = pages_hbm.shape[0]
+    load_pages = pltpu.make_async_copy(pages_hbm, pages, w_sems.at[2])
+    load_pages.start()
 
     def other(axis, by, flip):
         return device_at(shifted(place, axis, by), lax.rem(core + flip, 2))
@@ -146,6 +88,37 @@
     def columns(start, count):
         return pl.ds(start * 128, count * 128)
 
+    partner = other(2, 2, 0)
+    list_copy = send(shed_list, wanted_list, shed_sems.at[0], shed_sems.at[1], partner)
+    loads = [
+        pltpu.make_async_copy(gate_up_hbm, gate_up, w_sems.at[0]),
+        pltpu.make_async_copy(down_hbm, down, w_sems.at[1]),
+    ]
+
+    lane16 = lax.rem(lax.broadcasted_iota(jnp.int32, (16, 128), 1), 16)
+    sub16 = lax.broadcasted_iota(jnp.int32, (16, 128), 0)
+    repeat = (lane16 == sub16).astype(bf16)
+    earlier = (sub16 < lane16).astype(bf16)
+    own_ids = ids[...].astype(f32)
+    id_rows = jnp.dot(own_ids.astype(bf16), repeat, preferred_element_type=f32)
+    gates_left = gate_in[...]
+    gate_rows = None
+    for _ in range(3):
+        piece = gates_left.astype(bf16)
+        term = jnp.dot(piece, repeat, preferred_element_type=f32)
+        gate_rows = term if gate_rows is None else gate_rows + term
+        gates_left = gates_left - piece.astype(f32)
+    expert_sub = lax.broadcasted_iota(jnp.int32, (128, 1), 0).astype(f32)
+    member = jnp.zeros((128, 16), f32)
+    for k in range(8):
+        member = jnp.where(own_ids[k : k + 1, :] == expert_sub, 1.0, member)
+    before = jnp.dot(member.astype(bf16), earlier, preferred_element_type=f32)
+    for k in range(8):
+        rank = jnp.sum(
+            jnp.where(id_rows[k : k + 1, :] == expert_sub, before, 0.0), axis=0, keepdims=True
+        )
+        codes[k : k + 1, :] = id_rows[k : k + 1, :] * 2.0 + rank
+    codes[8:16, :] = gate_rows
     code_copies = []
     for i, (axis, by, flip) in enumerate(
         [(0, 0, 1)] + [(a, b, f) for a in range(3) for b in (1, 2, 3) for f in (0, 1)]
@@ -153,21 +126,107 @@
         code_copies.append(
             send(codes, gathered.at[i], code_s.at[i], code_r.at[i], other(axis, by, flip))
         )
-    first_copies = []
-    for c, (r, start, count) in enumerate(CHUNKS):
-        axis = ROTATIONS[r][0]
-        copies = []
-        for s in range(1, PEERS):
-            copies.append(
-                send(
-                    normed.at[:, columns(start, count)],
-                    first.at[s, :, columns(start, count)],
-                    s1_s.at[c, s], s1_r.at[c, s],
-                    other(axis, s // 2, s % 2),
-                )
-            )
-        first_copies.append(copies)
-    first[0] = normed[...]
+
+    load_pages.wait()
+    for load in loads:
+        load.start()
+    list_copy.wait_recv()
+    to_scalar = pltpu.make_async_copy(wanted_list, wanted_scalar, w_sems.at[3])
+    to_scalar.start()
+    to_scalar.wait()
+    shed_copies = []
+    half = shed_out.shape[0] // 2
+    for part in range(2):
+        for i in range(part * half, part * half + half):
+            shed_out[i] = pages[wanted_scalar[0, i]]
+        span = pl.ds(part * half, half)
+        shed_copies.append(
+            send(
+                shed_out.at[span], shed_in.at[span],
+                shed_sems.at[2 + part], shed_sems.at[4 + part], partner,
+            )
+        )
+
+    scaling = 1.0 / math.sqrt(HEAD)
+    for g in range(GROUPS):
+        for h in range(GROUP_HEADS):
+            heads[g, h * ROWS : (h + 1) * ROWS, :] = queries[
+                :, (g * GROUP_HEADS + h) * HEAD : (g * GROUP_HEADS + h + 1) * HEAD
+            ]
+    extra[...] = jnp.zeros_like(extra)
+    extra[0:ROWS, :] = new_kv[...]
+    table = page_table[...].astype(f32)
+    diagonal = lax.broadcasted_iota(jnp.int32, (ROWS, ROWS), 0) == lax.broadcasted_iota(
+        jnp.int32, (ROWS, ROWS), 1
+    )
+    length = jnp.sum(
+        jnp.where(diagonal, lengths[...].astype(f32), 0.0), axis=1, keepdims=True
+    )
+    token = lax.broadcasted_iota(jnp.int32, (ROWS, TILE), 1)
+    token_page = lax.div(token, PAGE).astype(f32)
+    token_place = lax.rem(token, PAGE).astype(f32)
+
+    def allowed(first_page):
+        limit = jnp.zeros((ROWS, TILE), f32)
+        for j in range(table.shape[1]):
+            left = jnp.maximum(length - float(j * PAGE), 0.0)
+            limit = limit + jnp.where(table[:, j : j + 1] == token_page + first_page, left, 0.0)
+        return token_place < limit
+
+    def masked(values, mask):
+        width = values.shape[1]
+        values = values.reshape(GROUP_HEADS, ROWS, width)
+        return jnp.where(mask[None], values, masked_score).reshape(GROUP_HEADS * ROWS, width)
+
+    def dot_last(left, right):
+        return lax.dot_general(
+            left, right, (((1,), (1,)), ((), ())), preferred_element_type=f32
+        )
+
+    new_mask = lax.broadcasted_iota(jnp.int32, (ROWS, EXTRA), 0) == lax.broadcasted_iota(
+        jnp.int32, (ROWS, EXTRA), 1
+    )
+    for g in range(GROUPS):
+        keys = extra[:, g * HEAD : (g + 1) * HEAD]
+        values = masked(dot_last(heads[g], keys), new_mask)
+        extra_scores[g] = values
+        peak[g] = values
+    tiles = own_pages // TILE_PAGES
+
+    def score_tile(t, carry):
+        mask = allowed((t * TILE_PAGES).astype(f32))
+        for g in range(GROUPS):
+            keys = pages[pl.ds(t * TILE_PAGES, TILE_PAGES), :, g * HEAD : (g + 1) * HEAD]
+            values = masked(dot_last(heads[g], keys.reshape(TILE, HEAD)), mask)
+            scores[g, t] = values
+            peak[g] = jnp.maximum(peak[g], jnp.maximum(values[:, :128], values[:, 128:]))
+        return carry
+
+    lax.fori_loop(0, tiles, score_tile, 0)
+    tops = []
+    for g in range(GROUPS):
+        top = jnp.max(peak[g], axis=1, keepdims=True)
+        tops.append(top)
+        weights = jnp.exp((extra_scores[g] - top) * scaling)
+        weight_sum[g] = weights
+        values = extra[:, (GROUPS + g) * HEAD : (GROUPS + g + 1) * HEAD]
+        summed[g] = jnp.dot(weights.astype(bf16), values, preferred_element_type=f32)
+
+    def weigh_tile(t, carry):
+        for g in range(GROUPS):
+            weights = jnp.exp((scores[g, t] - tops[g]) * scaling)
+            weight_sum[g] += weights[:, :128] + weights[:, 128:]
+            values = pages[
+                pl.ds(t * TILE_PAGES, TILE_PAGES), :, (GROUPS + g) * HEAD : (GROUPS + g + 1) * HEAD
+            ]
+            summed[g] += jnp.dot(
+                weights.astype(bf16), values.reshape(TILE, HEAD), preferred_element_type=f32
+            )
+        return carry
+
+    lax.fori_loop(0, tiles, weigh_tile, 0)
+    sums = [jnp.sum(weight_sum[g], axis=1, keepdims=True) for g in range(GROUPS)]
+
     for copy in code_copies:
         copy.wait_recv()
 
@@ -200,6 +259,51 @@
             weight[r, part] = piece
             gates = gates - piece.astype(jnp.float32)
 
+
+    shed_mask = allowed(float(own_pages))
+    for copy in shed_copies:
+        copy.wait_recv()
+    square = jnp.zeros((ROWS, HEAD), f32)
+    for g in range(GROUPS):
+        keys = shed_in[:, :, g * HEAD : (g + 1) * HEAD].reshape(TILE, HEAD)
+        values = masked(dot_last(heads[g], keys), shed_mask)
+        top = jnp.maximum(tops[g], jnp.max(values, axis=1, keepdims=True))
+        again = jnp.exp((tops[g] - top) * scaling)
+        weights = jnp.exp((values - top) * scaling)
+        denominator = sums[g] * again + jnp.sum(weights, axis=1, keepdims=True)
+        values = shed_in[:, :, (GROUPS + g) * HEAD : (GROUPS + g + 1) * HEAD].reshape(TILE, HEAD)
+        total = summed[g] * again + jnp.dot(
+            weights.astype(bf16), values, preferred_element_type=f32
+        )
+        total = (total / denominator).astype(bf16)
+        for h in range(GROUP_HEADS):
+            span = pl.ds((g * GROUP_HEADS + h) * HEAD, HEAD)
+            part = total[h * ROWS : (h + 1) * ROWS, :]
+            attended[:, span] = part
+            joined = (residual[:, span].astype(f32) + part.astype(f32)).astype(bf16)
+            merged[:, span] = joined
+            joined = joined.astype(f32)
+            square = square + joined * joined
+    width = queries.shape[1]
+    mean = jnp.sum(square, axis=1, keepdims=True) * (1.0 / width)
+    inverse = lax.rsqrt(mean + epsilon)
+    normed[...] = (merged[...].astype(f32) * inverse * gain[...]).astype(bf16)
+
+    first_copies = []
+    for c, (r, start, count) in enumerate(CHUNKS):
+        axis = ROTATIONS[r][0]
+        copies = []
+        for s in range(1, PEERS):
+            copies.append(
+                send(
+                    normed.at[:, columns(start, count)],
+                    first.at[s, :, columns(start, count)],
+                    s1_s.at[c, s], s1_r.at[c, s],
+                    other(axis, s // 2, s % 2),
+                )
+            )
+        first_copies.append(copies)
+    first[0] = normed[...]
     second_copies = []
     for c, (r, start, count) in enumerate(CHUNKS):
         a1 = ROTATIONS[r][1]
@@ -326,7 +430,7 @@
             )
             total = piece if total is None else total + piece
         total = total.reshape(PEERS, 16, count * 128)
-        own_sum[:, cols] = total[0]
+        expert_sum[:, cols] = total[0]
         partial[1:, :, cols] = total[1:].astype(jnp.bfloat16)
         copies = []
         for s in range(1, PEERS):
@@ -341,17 +445,23 @@
         for copy in three_copies[c]:
             copy.wait_recv()
         cols = columns(start, count)
-        total = own_sum[:, cols]
+        total = expert_sum[:, cols]
         for s in range(1, PEERS):
             total = total + back_three[s, :, cols].astype(jnp.float32)
-        out[:, cols] = (merged[:, cols].astype(jnp.float32) + total).astype(jnp.bfloat16)
+        expert_sum[:, cols] = total
     for copy in sends:
         copy.wait_send()
 
 
-def routed_experts(normed, codes, merged, gate_up, down):
-    width = normed.shape[1]
+def local(
+    queries, new_kv, kv_pages, page_table, lengths, shed_slots, residual, norm_gain,
+    expert_ids, gate_weights, w_gate_up, w_down,
+):
+    rows, width = queries.shape
+    gate_up, down = w_gate_up[0], w_down[0]
     hidden_dim = down.shape[0]
+    pages, page, kv_width = kv_pages.shape
+    shed = shed_slots.shape[0]
     chunks = len(CHUNKS)
     bf16, f32 = jnp.bfloat16, jnp.float32
     vmem = pl.BlockSpec(memory_space=pltpu.VMEM)
@@ -359,12 +469,31 @@
     block = pltpu.VMEM((SIDE, SIDE, 16, width), bf16)
     peers = pltpu.VMEM((PEERS, 16, width), bf16)
     dma = pltpu.SemaphoreType.DMA
-    return pl.pallas_call(
-        routed_experts_kernel,
-        out_shape=jax.ShapeDtypeStruct(normed.shape, bf16),
-        in_specs=[vmem, vmem, vmem, hbm, hbm],
-        out_specs=vmem,
+    group_rows = GROUP_HEADS * ROWS
+    attended, merged, expert_sum = pl.pallas_call(
+        layer_kernel,
+        out_shape=(
+            jax.ShapeDtypeStruct((rows, width), bf16),
+            jax.ShapeDtypeStruct((rows, width), bf16),
+            jax.ShapeDtypeStruct((rows, width), f32),
+        ),
+        in_specs=[vmem, vmem, hbm, vmem, vmem, vmem, vmem, vmem, vmem, vmem, hbm, hbm],
+        out_specs=(vmem, vmem, vmem),
         scratch_shapes=[
+            pltpu.VMEM((pages, page, kv_width), bf16),
+            pltpu.VMEM((EXTRA, kv_width), bf16),
+            pltpu.VMEM((1, shed), jnp.int32),
+            pltpu.SMEM((1, shed), jnp.int32),
+            pltpu.VMEM((shed, page, kv_width), bf16),
+            pltpu.VMEM((shed, page, kv_width), bf16),
+            pltpu.VMEM((GROUPS, group_rows, HEAD), bf16),
+            pltpu.VMEM((GROUPS, pages // TILE_PAGES, group_rows, TILE), f32),
+            pltpu.VMEM((GROUPS, group_rows, EXTRA), f32),
+            pltpu.VMEM((GROUPS, group_rows, 128), f32),
+            pltpu.VMEM((GROUPS, group_rows, 128), f32),
+            pltpu.VMEM((GROUPS, group_rows, HEAD), f32),
+            pltpu.VMEM((rows, width), bf16),
+            pltpu.VMEM((16, 128), f32),
             pltpu.VMEM(gate_up.shape, bf16),
             pltpu.VMEM(down.shape, bf16),
             pltpu.VMEM((19, 16, 128), f32),
@@ -380,9 +509,9 @@
             block,
             block,
             peers,
-            pltpu.VMEM((16, width), f32),
             peers,
-            dma((2,)),
+            dma((4,)),
+            dma((6,)),
             dma((19,)), dma((19,)),
             dma((chunks, PEERS)), dma((chunks, PEERS)),
             dma((chunks, SIDE)), dma((chunks, SIDE)),
@@ -394,53 +523,12 @@
         compiler_params=pltpu.CompilerParams(
             collective_id=0, has_side_effects=True, vmem_limit_bytes=60 * 1024 * 1024
         ),
-    )(normed, codes, merged, gate_up, down)
-
-
-def local(
-    queries,
-    new_kv,
-    kv_pages,
-    page_table,
-    lengths,
-    shed_slots,
-    residual,
-    norm_gain,
-    expert_ids,
-    gate_weights,
-    w_gate_up,
-    w_down,
-):
-    count_of_rows, model_dim = queries.shape
-    pages_own, page_len, kv_width = kv_pages.shape
-    table_width = page_table.shape[1]
-    query_head_block = queries.reshape(
-        count_of_rows, KEY_VALUE_HEADS, QUERY_GROUP_SIZE, HEAD_DIMENSION
-    )
-    scaling = 1.0 / math.sqrt(HEAD_DIMENSION)
-    positions = jnp.arange(table_width * page_len, dtype=jnp.int32)
-    allowed = positions[None, :] < lengths[:, None]
-    requested = from_behind(shed_slots, "pool", 1)
-    fetched = from_behind(jnp.take(kv_pages, requested, axis=0), "pool", 1)
-    combined = jnp.concatenate([kv_pages, fetched], axis=0)
-    scores, value_entries = cache_scores(combined, page_table, allowed, query_head_block, scaling)
-    attended = finish_attention([scores], [value_entries], query_head_block, new_kv, scaling)
-    merged = (residual.astype(jnp.float32) + attended.astype(jnp.float32)).astype(jnp.bfloat16)
-    merged_wide = merged.astype(jnp.float32)
-    normed = (
-        merged_wide
-        * lax.rsqrt(jnp.mean(merged_wide * merged_wide, axis=-1, keepdims=True) + epsilon)
-        * norm_gain
-    ).astype(jnp.bfloat16)
-    same = expert_ids[:, :, None, None] == expert_ids[None, None, :, :]
-    row_index = jnp.arange(count_of_rows, dtype=jnp.int32)
-    before = row_index[:, None, None, None] > row_index[None, None, :, None]
-    slot_rank = jnp.sum((same & before).astype(jnp.int32), axis=(2, 3))
-    codes = jnp.concatenate(
-        [(expert_ids * 2 + slot_rank).astype(jnp.float32).T, gate_weights.T], axis=0
-    )
-    codes = jnp.tile(codes, (1, PEERS))
-    layer_out = routed_experts(normed, codes, merged, w_gate_up[0], w_down[0])
+    )(
+        queries, new_kv, kv_pages, page_table, lengths.reshape(1, rows),
+        shed_slots.reshape(1, shed), residual, norm_gain.reshape(1, width),
+        expert_ids.T, gate_weights.T, gate_up, down,
+    )
+    layer_out = (merged.astype(f32) + expert_sum).astype(bf16)
     return (attended, layer_out)
 
 

time: 109 us -> 80.5 us (0.74)
  local copies, waits for them, and re-layouts: 18.5 us -> 1.57 us
  Pallas kernels: 64 us -> 76.5 us
  other arithmetic: 12.6 us -> 1.66 us
  waiting for transfers between devices: 6.27 us -> 0 us
  starting transfers between devices: 4.59 us -> 0 us
  matrix products: 1.36 us -> 0 us
    pallas_call x1, Pallas kernels: 64 us -> 76.5 us  [local(): pl.pallas_call(layer_kernel, out_shape=(jax.ShapeDtypeStruct((rows, width...]
    slice x3 -> x0, local copies, waits for them, and re-layouts: 8.34 us -> none  [the longest x2 5.3 us: cache_scores(): collected_rows[:, :, :key_row_width]]
    ppermute x2 -> x0, waiting for transfers between devices: 6.27 us -> none  [from_behind(): lax.ppermute(value, axis, [(i, (i + by) % length) for i in range(length)])]
    gather x2 -> x0, local copies, waits for them, and re-layouts: 4.9 us -> none  [the longest x1 2.75 us: cache_scores(): jnp.take(source, index_table, axis=0)]
    ppermute x2 -> x0, starting transfers between devices: 4.59 us -> none  [from_behind(): lax.ppermute(value, axis, [(i, (i + by) % length) for i in range(length)])]
    reduce_sum x3 -> x0, other arithmetic: 4.34 us -> none  [the longest x1 3.22 us: local(): slot_rank = jnp.sum((same & before).astype(jnp.int32), axis=(2, 3))]
    select_n x4 -> x0, other arithmetic: 3.37 us -> none  [the longest x2 3.28 us: cache_scores(): jnp.take(source, index_table, axis=0)]
    unnamed x10 -> x1, local copies, waits for them, and re-layouts: 4.2 us -> 1.57 us
  transfers between devices with their start and end apart: 2 -> 0, of which waited for: 1 -> 0; matrix products, arithmetic and copies ran while one was open for 9% -> 0% of each run, Pallas kernels for 0% -> 0%
where the time goes in v2:
time: 80.5 us; the launch traced here: 80.4 us
  Pallas kernels  76.5 us (95%)
  other arithmetic  1.66 us (2%)
  local copies, waits for them, and re-layouts  1.57 us (2%)
    pallas_call x1, Pallas kernels, local(): pl.pallas_call(layer_kernel, out_shape=(jax.ShapeDtypeStruct((rows, width...  76.5 us
    convert_element_type x1, other arithmetic, local(): layer_out = (merged.astype(f32) + expert_sum).astype(bf16)  1.66 us

profile of v2, /device:TPU:1, one launch (start us, length us, event | category | flops | bytes accessed | tf_op | source)
XLA Modules:
  0.0 80.4 jit_solution(7952896583576448776)
XLA Ops:
  0.6 76.5 %shard_map.131 = (bf16[16,4096]{1,0:T(8,128)(2,1)}, bf16[16,4096]{1,0:T(8,128)(2,1)}, f32[16,4096]{1,0:T(8,128)}) custom-call(bf16[16,4096]{1,0:T(8,128)(2,1)} %queries.1, bf16[16,512]{1,0:T(8,128)(2,1)} %new_kv.1, bf16[128,16,512]{2,1,0:T(8,128)(2,1)} %pages_hbm.1, s32[16,16]{1,0:T(8,128)} %page_table.1, s32[1,16]{1,0:T(1,128)} %bitcast.12, ...), custom_call_target="tpu_custom_call" | custom-call | tf_op jit(solution)/shard_map/pallas_call | solution.py:473
  77.1 1.7 %add_convert_fusion = bf16[16,4096]{1,0:T(8,128)(2,1)} fusion(f32[16,4096]{1,0:T(8,128)} %get-tuple-element.7, bf16[16,4096]{1,0:T(8,128)(2,1)} %get-tuple-element.6), kind=kLoop, calls=%fused_computation | loop fusion | flops 196608 | bytes 524288 | tf_op jit(solution)/shard_map/convert_element_type | solution.py:531
  78.8 1.6 %copy.15 = bf16[16,4096]{1,0:T(8,128)(2,1)} copy(bf16[16,4096]{1,0:T(8,128)(2,1)} %get-tuple-element.10) | data formatting | bytes 262144

commit v3 on v2

--- a/solution.py
+++ b/solution.py
@@ -47,21 +47,32 @@
 
 
 def layer_kernel(
-    queries, new_kv, pages_hbm, page_table, lengths, shed_list, residual, gain, ids, gate_in,
-    gate_up_hbm, down_hbm, attended, merged, expert_sum,
+    queries_hbm, new_kv_hbm, pages_hbm, page_table_hbm, lengths_hbm, shed_list, residual_hbm,
+    gain_hbm, ids_hbm, gate_in_hbm, gate_up_hbm, down_hbm, attended_out, layer_out,
+    queries, new_kv, page_table, lengths, residual, gain, ids, gate_in,
+    attended, merged, expert_sum,
     pages, extra, wanted_list, wanted_scalar, shed_out, shed_in, heads, scores, extra_scores,
     peak, weight_sum, summed, normed, codes,
     gate_up, down, gathered, select, weight, first, packed, second, third, product, hidden,
     sent_back, back_one, back_two, partial, back_three,
-    w_sems, shed_sems, code_s, code_r, s1_s, s1_r, s2_s, s2_r, s3_s, s3_r,
-    r3_s, r3_r, r2_s, r2_r, r1_s, r1_r,
+    w_sems, in_sems, shed_sems, code_sems, sent, s1_r, s2_r, s3_r, r3_r, r2_r, r1_r,
 ):
     bf16, f32 = jnp.bfloat16, jnp.float32
     place, core = coordinates()
     hidden_dim = down.shape[0]
     own_pages = pages_hbm.shape[0]
     load_pages = pltpu.make_async_copy(pages_hbm, pages, w_sems.at[2])
-    load_pages.start()
+    inputs = []
+    for i, (source, target) in enumerate(
+        (
+            (ids_hbm, ids), (gate_in_hbm, gate_in), (page_table_hbm, page_table),
+            (lengths_hbm, lengths), (queries_hbm, queries), (new_kv_hbm, new_kv),
+            (residual_hbm, residual), (gain_hbm, gain),
+        )
+    ):
+        inputs.append(pltpu.make_async_copy(source, target, in_sems.at[i]))
+    for load in inputs[:2] + [load_pages] + inputs[2:]:
+        load.start()
 
     def other(axis, by, flip):
         return device_at(shifted(place, axis, by), lax.rem(core + flip, 2))
@@ -74,27 +85,28 @@
         pl.semaphore_signal(barrier, inc=1, device_id=neighbour, device_id_type=MESH_ID)
     pl.semaphore_wait(barrier, len(neighbours))
 
-    sends = []
-
     def send(source, target, send_sem, recv_sem, device):
         copy = pltpu.make_async_remote_copy(
             src_ref=source, dst_ref=target, send_sem=send_sem, recv_sem=recv_sem,
             device_id=device, device_id_type=MESH_ID,
         )
         copy.start()
-        sends.append(copy)
-        return copy
+
+    def settle(region, sem):
+        pltpu.make_async_copy(region, region, sem).wait()
 
     def columns(start, count):
         return pl.ds(start * 128, count * 128)
 
     partner = other(2, 2, 0)
-    list_copy = send(shed_list, wanted_list, shed_sems.at[0], shed_sems.at[1], partner)
+    send(shed_list, wanted_list, shed_sems.at[0], shed_sems.at[1], partner)
     loads = [
         pltpu.make_async_copy(gate_up_hbm, gate_up, w_sems.at[0]),
         pltpu.make_async_copy(down_hbm, down, w_sems.at[1]),
     ]
 
+    for load in inputs[:2]:
+        load.wait()
     lane16 = lax.rem(lax.broadcasted_iota(jnp.int32, (16, 128), 1), 16)
     sub16 = lax.broadcasted_iota(jnp.int32, (16, 128), 0)
     repeat = (lane16 == sub16).astype(bf16)
@@ -119,34 +131,27 @@
         )
         codes[k : k + 1, :] = id_rows[k : k + 1, :] * 2.0 + rank
     codes[8:16, :] = gate_rows
-    code_copies = []
     for i, (axis, by, flip) in enumerate(
         [(0, 0, 1)] + [(a, b, f) for a in range(3) for b in (1, 2, 3) for f in (0, 1)]
     ):
-        code_copies.append(
-            send(codes, gathered.at[i], code_s.at[i], code_r.at[i], other(axis, by, flip))
-        )
+        send(codes, gathered.at[i], code_sems.at[0], code_sems.at[1], other(axis, by, flip))
 
     load_pages.wait()
     for load in loads:
         load.start()
-    list_copy.wait_recv()
+    settle(wanted_list, shed_sems.at[1])
     to_scalar = pltpu.make_async_copy(wanted_list, wanted_scalar, w_sems.at[3])
     to_scalar.start()
     to_scalar.wait()
-    shed_copies = []
     half = shed_out.shape[0] // 2
     for part in range(2):
         for i in range(part * half, part * half + half):
             shed_out[i] = pages[wanted_scalar[0, i]]
         span = pl.ds(part * half, half)
-        shed_copies.append(
-            send(
-                shed_out.at[span], shed_in.at[span],
-                shed_sems.at[2 + part], shed_sems.at[4 + part], partner,
-            )
-        )
-
+        send(shed_out.at[span], shed_in.at[span], shed_sems.at[2], shed_sems.at[3], partner)
+
+    for load in inputs[2:]:
+        load.wait()
     scaling = 1.0 / math.sqrt(HEAD)
     for g in range(GROUPS):
         for h in range(GROUP_HEADS):
@@ -227,8 +232,7 @@
     lax.fori_loop(0, tiles, weigh_tile, 0)
     sums = [jnp.sum(weight_sum[g], axis=1, keepdims=True) for g in range(GROUPS)]
 
-    for copy in code_copies:
-        copy.wait_recv()
+    settle(gathered, code_sems.at[1])
 
     row = lax.broadcasted_iota(jnp.int32, (256, 1), 0)
     lane = lax.broadcasted_iota(jnp.int32, (1, 128), 1)
@@ -261,8 +265,7 @@
 
 
     shed_mask = allowed(float(own_pages))
-    for copy in shed_copies:
-        copy.wait_recv()
+    settle(shed_in, shed_sems.at[3])
     square = jnp.zeros((ROWS, HEAD), f32)
     for g in range(GROUPS):
         keys = shed_in[:, :, g * HEAD : (g + 1) * HEAD].reshape(TILE, HEAD)
@@ -284,63 +287,48 @@
             merged[:, span] = joined
             joined = joined.astype(f32)
             square = square + joined * joined
+    write_attended = pltpu.make_async_copy(attended, attended_out, w_sems.at[4])
+    write_attended.start()
     width = queries.shape[1]
     mean = jnp.sum(square, axis=1, keepdims=True) * (1.0 / width)
     inverse = lax.rsqrt(mean + epsilon)
     normed[...] = (merged[...].astype(f32) * inverse * gain[...]).astype(bf16)
 
-    first_copies = []
     for c, (r, start, count) in enumerate(CHUNKS):
         axis = ROTATIONS[r][0]
-        copies = []
         for s in range(1, PEERS):
-            copies.append(
-                send(
-                    normed.at[:, columns(start, count)],
-                    first.at[s, :, columns(start, count)],
-                    s1_s.at[c, s], s1_r.at[c, s],
-                    other(axis, s // 2, s % 2),
-                )
-            )
-        first_copies.append(copies)
+            send(
+                normed.at[:, columns(start, count)],
+                first.at[s, :, columns(start, count)],
+                sent.at[0], s1_r.at[c],
+                other(axis, s // 2, s % 2),
+            )
     first[0] = normed[...]
-    second_copies = []
     for c, (r, start, count) in enumerate(CHUNKS):
         a1 = ROTATIONS[r][1]
-        for copy in first_copies[c]:
-            copy.wait_recv()
+        settle(first.at[pl.ds(1, PEERS - 1), :, columns(start, count)], s1_r.at[c])
         cols = columns(start, count)
         rows = first[:, :, cols].reshape(PEERS * 16, count * 128)
         block = jnp.dot(select[r], rows, preferred_element_type=jnp.float32).astype(jnp.bfloat16)
         block = block.reshape(SIDE, SIDE, 16, count * 128)
         second[0, :, :, cols] = block[0]
-        copies = []
         for d in (2, 1, 3):
             packed[d, :, :, cols] = block[d]
         for d in (2, 1, 3):
-            copies.append(
-                send(
-                    packed.at[d, :, :, cols], second.at[d, :, :, cols],
-                    s2_s.at[c, d], s2_r.at[c, d], other(a1, d, 0),
-                )
-            )
-        second_copies.append(copies)
-    third_copies = []
+            send(
+                packed.at[d, :, :, cols], second.at[d, :, :, cols],
+                sent.at[1], s2_r.at[c], other(a1, d, 0),
+            )
     for c, (r, start, count) in enumerate(CHUNKS):
         a2 = ROTATIONS[r][2]
-        for copy in second_copies[c]:
-            copy.wait_recv()
-        cols = columns(start, count)
-        copies = []
+        settle(second.at[pl.ds(1, SIDE - 1), :, :, columns(start, count)], s2_r.at[c])
+        cols = columns(start, count)
         for d in (2, 1, 3):
-            copies.append(
-                send(
-                    second.at[:, d, :, cols], third.at[d, :, :, cols],
-                    s3_s.at[c, d], s3_r.at[c, d], other(a2, d, 0),
-                )
+            send(
+                second.at[:, d, :, cols], third.at[d, :, :, cols],
+                sent.at[2], s3_r.at[c], other(a2, d, 0),
             )
         third[0, :, :, cols] = second[:, 0, :, cols]
-        third_copies.append(copies)
 
     canon = lax.broadcasted_iota(jnp.int32, (256, 256), 0)
     local = lax.broadcasted_iota(jnp.int32, (256, 256), 1)
@@ -356,8 +344,7 @@
 
     loads[0].wait()
     for c, (r, start, count) in enumerate(CHUNKS):
-        for copy in third_copies[c]:
-            copy.wait_recv()
+        settle(third.at[pl.ds(1, SIDE - 1), :, :, columns(start, count)], s3_r.at[c])
         cols = columns(start, count)
         tokens = third[:, :, :, cols].reshape(256, count * 128)
         if r:
@@ -381,7 +368,6 @@
         hidden[r] = turned.astype(jnp.bfloat16)
 
     loads[1].wait()
-    one_copies = []
     for c, (r, start, count) in enumerate(CHUNKS):
         a2 = ROTATIONS[r][2]
         cols = columns(start, count)
@@ -390,36 +376,24 @@
         back_one[0, :, :, cols] = finished[0]
         for d in (2, 1, 3):
             sent_back[d, :, :, cols] = finished[d]
-        copies = []
         for d in (2, 1, 3):
-            copies.append(
-                send(
-                    sent_back.at[d, :, :, cols], back_one.at[d, :, :, cols],
-                    r3_s.at[c, d], r3_r.at[c, d], other(a2, -d, 0),
-                )
-            )
-        one_copies.append(copies)
-    two_copies = []
+            send(
+                sent_back.at[d, :, :, cols], back_one.at[d, :, :, cols],
+                sent.at[3], r3_r.at[c], other(a2, -d, 0),
+            )
     for c, (r, start, count) in enumerate(CHUNKS):
         a1 = ROTATIONS[r][1]
-        for copy in one_copies[c]:
-            copy.wait_recv()
-        cols = columns(start, count)
-        copies = []
+        settle(back_one.at[pl.ds(1, SIDE - 1), :, :, columns(start, count)], r3_r.at[c])
+        cols = columns(start, count)
         for d in (2, 1, 3):
-            copies.append(
-                send(
-                    back_one.at[:, d, :, cols], back_two.at[d, :, :, cols],
-                    r2_s.at[c, d], r2_r.at[c, d], other(a1, -d, 0),
-                )
+            send(
+                back_one.at[:, d, :, cols], back_two.at[d, :, :, cols],
+                sent.at[4], r2_r.at[c], other(a1, -d, 0),
             )
         back_two[0, :, :, cols] = back_one[:, 0, :, cols]
-        two_copies.append(copies)
-    three_copies = []
     for c, (r, start, count) in enumerate(CHUNKS):
         a0 = ROTATIONS[r][0]
-        for copy in two_copies[c]:
-            copy.wait_recv()
+        settle(back_two.at[pl.ds(1, SIDE - 1), :, :, columns(start, count)], r2_r.at[c])
         cols = columns(start, count)
         results = back_two[:, :, :, cols].reshape(256, count * 128)
         total = None
@@ -432,25 +406,33 @@
         total = total.reshape(PEERS, 16, count * 128)
         expert_sum[:, cols] = total[0]
         partial[1:, :, cols] = total[1:].astype(jnp.bfloat16)
-        copies = []
         for s in range(1, PEERS):
-            copies.append(
-                send(
-                    partial.at[s, :, cols], back_three.at[s, :, cols],
-                    r1_s.at[c, s], r1_r.at[c, s], other(a0, -(s // 2), s % 2),
-                )
-            )
-        three_copies.append(copies)
-    for c, (r, start, count) in enumerate(CHUNKS):
-        for copy in three_copies[c]:
-            copy.wait_recv()
+            send(
+                partial.at[s, :, cols], back_three.at[s, :, cols],
+                sent.at[5], r1_r.at[c], other(a0, -(s // 2), s % 2),
+            )
+    for c, (r, start, count) in enumerate(CHUNKS):
+        settle(back_three.at[pl.ds(1, PEERS - 1), :, columns(start, count)], r1_r.at[c])
         cols = columns(start, count)
         total = expert_sum[:, cols]
         for s in range(1, PEERS):
             total = total + back_three[s, :, cols].astype(jnp.float32)
-        expert_sum[:, cols] = total
-    for copy in sends:
-        copy.wait_send()
+        merged[:, cols] = (merged[:, cols].astype(jnp.float32) + total).astype(jnp.bfloat16)
+    write_layer = pltpu.make_async_copy(merged, layer_out, w_sems.at[5])
+    write_layer.start()
+    settle(shed_list, shed_sems.at[0])
+    settle(gathered, code_sems.at[0])
+    settle(shed_out, shed_sems.at[2])
+    for i, region in enumerate(
+        (
+            first.at[pl.ds(1, PEERS - 1)], packed.at[pl.ds(1, SIDE - 1)],
+            third.at[pl.ds(1, SIDE - 1)], sent_back.at[pl.ds(1, SIDE - 1)],
+            back_two.at[pl.ds(1, SIDE - 1)], partial.at[pl.ds(1, PEERS - 1)],
+        )
+    ):
+        settle(region, sent.at[i])
+    write_attended.wait()
+    write_layer.wait()
 
 
 def local(
@@ -464,22 +446,31 @@
     shed = shed_slots.shape[0]
     chunks = len(CHUNKS)
     bf16, f32 = jnp.bfloat16, jnp.float32
-    vmem = pl.BlockSpec(memory_space=pltpu.VMEM)
     hbm = pl.BlockSpec(memory_space=pl.ANY)
     block = pltpu.VMEM((SIDE, SIDE, 16, width), bf16)
     peers = pltpu.VMEM((PEERS, 16, width), bf16)
     dma = pltpu.SemaphoreType.DMA
     group_rows = GROUP_HEADS * ROWS
-    attended, merged, expert_sum = pl.pallas_call(
+    attended, layer_out = pl.pallas_call(
         layer_kernel,
         out_shape=(
             jax.ShapeDtypeStruct((rows, width), bf16),
             jax.ShapeDtypeStruct((rows, width), bf16),
-            jax.ShapeDtypeStruct((rows, width), f32),
         ),
-        in_specs=[vmem, vmem, hbm, vmem, vmem, vmem, vmem, vmem, vmem, vmem, hbm, hbm],
-        out_specs=(vmem, vmem, vmem),
+        in_specs=[hbm] * 12,
+        out_specs=(hbm, hbm),
         scratch_shapes=[
+            pltpu.VMEM((rows, width), bf16),
+            pltpu.VMEM((rows, kv_width), bf16),
+            pltpu.VMEM(page_table.shape, jnp.int32),
+            pltpu.VMEM((1, rows), jnp.int32),
+            pltpu.VMEM((rows, width), bf16),
+            pltpu.VMEM((1, width), f32),
+            pltpu.VMEM((8, rows), jnp.int32),
+            pltpu.VMEM((8, rows), f32),
+            pltpu.VMEM((rows, width), bf16),
+            pltpu.VMEM((rows, width), bf16),
+            pltpu.VMEM((rows, width), f32),
             pltpu.VMEM((pages, page, kv_width), bf16),
             pltpu.VMEM((EXTRA, kv_width), bf16),
             pltpu.VMEM((1, shed), jnp.int32),
@@ -510,25 +501,23 @@
             block,
             peers,
             peers,
-            dma((4,)),
-            dma((6,)),
-            dma((19,)), dma((19,)),
-            dma((chunks, PEERS)), dma((chunks, PEERS)),
-            dma((chunks, SIDE)), dma((chunks, SIDE)),
-            dma((chunks, SIDE)), dma((chunks, SIDE)),
-            dma((chunks, SIDE)), dma((chunks, SIDE)),
-            dma((chunks, SIDE)), dma((chunks, SIDE)),
-            dma((chunks, PEERS)), dma((chunks, PEERS)),
+            dma((6,)), dma((8,)), dma((4,)), dma((2,)), dma((6,)),
+            dma((chunks,)), dma((chunks,)), dma((chunks,)),
+            dma((chunks,)), dma((chunks,)), dma((chunks,)),
         ],
         compiler_params=pltpu.CompilerParams(
-            collective_id=0, has_side_effects=True, vmem_limit_bytes=60 * 1024 * 1024
+            collective_id=0, has_side_effects=True, vmem_limit_bytes=52 * 1024 * 1024
         ),
     )(
-        queries, new_kv, kv_pages, page_table, lengths.reshape(1, rows),
-        shed_slots.reshape(1, shed), residual, norm_gain.reshape(1, width),
-        expert_ids.T, gate_weights.T, gate_up, down,
-    )
-    layer_out = (merged.astype(f32) + expert_sum).astype(bf16)
+        *(
+            pltpu.with_memory_space_constraint(value, pltpu.HBM)
+            for value in (
+                queries, new_kv, kv_pages, page_table, lengths.reshape(1, rows),
+                shed_slots.reshape(1, shed), residual, norm_gain.reshape(1, width),
+                expert_ids.T, gate_weights.T, gate_up, down,
+            )
+        )
+    )
     return (attended, layer_out)
 
 

time: 80.5 us -> 74 us (0.919)
  Pallas kernels: 76.5 us -> 72 us
  other arithmetic: 1.66 us -> 0 us
    pallas_call x1, Pallas kernels: 76.5 us -> 72 us  [local(): pl.pallas_call(layer_kernel, out_shape=(jax.ShapeDtypeStruct((rows, width...]
    convert_element_type x1 -> x0, other arithmetic: 1.66 us -> none  [local(): layer_out = (merged.astype(f32) + expert_sum).astype(bf16)]
where the time goes in v3:
time: 74 us; the launch traced here: 73.9 us
  Pallas kernels  72 us (97%)
  local copies, waits for them, and re-layouts  1.31 us (2%)
    pallas_call x1, Pallas kernels, local(): pl.pallas_call(layer_kernel, out_shape=(jax.ShapeDtypeStruct((rows, width...  72 us

profile of v3, /device:TPU:1, one launch (start us, length us, event | category | flops | bytes accessed | tf_op | source)
XLA Modules:
  0.0 73.9 jit_solution(15221652893468909722)
XLA Ops:
  0.6 72.0 %shard_map.131 = (bf16[16,4096]{1,0:T(8,128)(2,1)S(1)}, bf16[16,4096]{1,0:T(8,128)(2,1)S(1)}) custom-call(bf16[16,4096]{1,0:T(8,128)(2,1)} %queries_hbm.1, bf16[16,512]{1,0:T(8,128)(2,1)} %new_kv_hbm.1, bf16[128,16,512]{2,1,0:T(8,128)(2,1)} %pages_hbm.1, s32[16,16]{1,0:T(8,128)} %page_table_hbm.1, s32[1,16]{1,0:T(1,128)} %bitcast.12, s32[1,16]{1,0:T(1,128)} %bitcast.13, ...), custom_call_target="tpu_custom_call" | custom-call | tf_op jit(solution)/shard_map/pallas_call | solution.py:454
  72.6 0.7 copy.16
  73.3 0.7 copy.17

commit v4 on v3

--- a/solution.py
+++ b/solution.py
@@ -20,10 +20,18 @@
 epsilon = 1e-06
 
 MESH_ID = pl.DeviceIdType.MESH
+AHEAD = 3
+BEHIND = 1
+EARLY = 6
+LATE = 3
 ROTATIONS = ((0, 1, 2), (1, 2, 0), (2, 0, 1))
 SIDE = 4
 PEERS = 8
-CHUNKS = ((0, 0, 6), (1, 6, 5), (2, 11, 5), (0, 16, 5), (1, 21, 6), (2, 27, 5))
+CHUNKS = (
+    (0, 0, 4), (1, 4, 4), (2, 8, 4),
+    (0, 12, 4), (1, 16, 4), (2, 20, 4),
+    (0, 24, 3), (1, 27, 3), (2, 30, 2),
+)
 
 
 def coordinates():
@@ -53,9 +61,10 @@
     attended, merged, expert_sum,
     pages, extra, wanted_list, wanted_scalar, shed_out, shed_in, heads, scores, extra_scores,
     peak, weight_sum, summed, normed, codes,
-    gate_up, down, gathered, select, weight, first, packed, second, third, product, hidden,
-    sent_back, back_one, back_two, partial, back_three,
-    w_sems, in_sems, shed_sems, code_sems, sent, s1_r, s2_r, s3_r, r3_r, r2_r, r1_r,
+    gate_up, down, gathered, select, weight, first, packed, second, third, tokens, product, hidden,
+    sent_back, back_one, back_two, partial, near_sum, from_core, back_three,
+    w_sems, in_sems, shed_sems, code_sems, sent, core_sems, s1_r, s2_r, s3_r,
+    r3_r, r2_r, r1_r, forward_r, core_r,
 ):
     bf16, f32 = jnp.bfloat16, jnp.float32
     place, core = coordinates()
@@ -242,9 +251,12 @@
     lane_peer = lax.div(lax.broadcasted_iota(jnp.int32, (16, 128), 1), 16)
     for r, (a0, a1, a2) in enumerate(ROTATIONS):
         entries = jnp.where(lane_peer == 0, codes[...], 0.0)
-        entries = jnp.where(lane_peer == 1, gathered[0], entries)
-        for s in range(2, PEERS):
-            entries = jnp.where(lane_peer == s, gathered[1 + a0 * 6 + s - 2], entries)
+        entries = jnp.where(lane_peer == SIDE, gathered[0], entries)
+        for d in range(1, SIDE):
+            for flip in (0, 1):
+                entries = jnp.where(
+                    lane_peer == flip * SIDE + d, gathered[a0 * 6 + d * 2 - 1 + flip], entries
+                )
         where = list(place)
         where[a1] = lax.rem(place[a1] + lax.div(row, 64), SIDE)
         where[a2] = lax.rem(place[a2] + lax.rem(lax.div(row, 16), SIDE), SIDE)
@@ -258,9 +270,10 @@
             chosen = jnp.where(match, 1.0, chosen)
             gates = jnp.where(match, entries[8 + k : 9 + k, :], gates)
         select[r] = chosen.astype(jnp.bfloat16)
+        gates = gates.T
         for part in range(3):
             piece = gates.astype(jnp.bfloat16)
-            weight[r, part] = piece
+            weight[r, part * 128 : (part + 1) * 128, :] = piece
             gates = gates - piece.astype(jnp.float32)
 
 
@@ -294,19 +307,41 @@
     inverse = lax.rsqrt(mean + epsilon)
     normed[...] = (merged[...].astype(f32) * inverse * gain[...]).astype(bf16)
 
+    sibling = other(0, 0, 1)
+    send(normed, first.at[SIDE], core_sems.at[0], core_sems.at[1], sibling)
     for c, (r, start, count) in enumerate(CHUNKS):
-        axis = ROTATIONS[r][0]
-        for s in range(1, PEERS):
+        cols = columns(start, count)
+        for d in (2, 1, 3):
             send(
-                normed.at[:, columns(start, count)],
-                first.at[s, :, columns(start, count)],
-                sent.at[0], s1_r.at[c],
-                other(axis, s // 2, s % 2),
-            )
+                normed.at[:, cols], first.at[d, :, cols],
+                sent.at[0], s1_r.at[c], other(ROTATIONS[r][0], d, 0),
+            )
+            if c < EARLY:
+                send(
+                    normed.at[:, cols], first.at[SIDE + d, :, cols],
+                    core_sems.at[4], forward_r.at[c], other(ROTATIONS[r][0], d, 1),
+                )
     first[0] = normed[...]
+
+    def forward(c):
+        cols = columns(*CHUNKS[c][1:])
+        near = first.at[pl.ds(1, SIDE - 1), :, cols]
+        settle(near, s1_r.at[c])
+        if c < EARLY:
+            return
+        send(
+            near, first.at[pl.ds(SIDE + 1, SIDE - 1), :, cols],
+            core_sems.at[2], forward_r.at[c], sibling,
+        )
+
+    settle(first.at[SIDE], core_sems.at[1])
     for c, (r, start, count) in enumerate(CHUNKS):
         a1 = ROTATIONS[r][1]
-        settle(first.at[pl.ds(1, PEERS - 1), :, columns(start, count)], s1_r.at[c])
+        if c < EARLY:
+            forward(c)
+        if EARLY <= c + AHEAD < len(CHUNKS):
+            forward(c + AHEAD)
+        settle(first.at[pl.ds(SIDE + 1, SIDE - 1), :, columns(start, count)], forward_r.at[c])
         cols = columns(start, count)
         rows = first[:, :, cols].reshape(PEERS * 16, count * 128)
         block = jnp.dot(select[r], rows, preferred_element_type=jnp.float32).astype(jnp.bfloat16)
@@ -333,29 +368,35 @@
     canon = lax.broadcasted_iota(jnp.int32, (256, 256), 0)
     local = lax.broadcasted_iota(jnp.int32, (256, 256), 1)
     apart = (
-        lax.rem(lax.div(canon, 4), SIDE),
+        lax.rem(lax.div(canon, 2), SIDE),
         lax.rem(lax.div(canon, 16), SIDE),
         lax.div(canon, 64),
     )
+    flip = lax.rem(lax.div(canon, 8), 2) * 8
     orders = []
     for a0, a1, a2 in ROTATIONS:
-        index = apart[a2] * 64 + apart[a1] * 16 + apart[a0] * 4 + lax.rem(canon, 4)
+        index = apart[a2] * 64 + apart[a1] * 16 + apart[a0] * 2 + lax.rem(canon, 2) + flip
         orders.append((index == local).astype(jnp.bfloat16))
 
     loads[0].wait()
     for c, (r, start, count) in enumerate(CHUNKS):
-        settle(third.at[pl.ds(1, SIDE - 1), :, :, columns(start, count)], s3_r.at[c])
-        cols = columns(start, count)
-        tokens = third[:, :, :, cols].reshape(256, count * 128)
+        cols = columns(start, count)
+        settle(third.at[pl.ds(1, SIDE - 1), :, :, cols], s3_r.at[c])
+        rows = third[:, :, :, cols].reshape(256, count * 128)
         if r:
-            tokens = jnp.dot(orders[r], tokens, preferred_element_type=jnp.float32)
-            tokens = tokens.astype(jnp.bfloat16)
+            rows = jnp.dot(orders[r], rows, preferred_element_type=jnp.float32)
+            rows = rows.astype(jnp.bfloat16)
+        tokens[:, cols] = rows
+        if r < 2:
+            continue
+        begin = CHUNKS[c - 2][1]
+        span = columns(begin, start + count - begin)
         for n in range(0, 2 * hidden_dim, 512):
             piece = jnp.dot(
-                tokens, gate_up[pl.ds(start * 128, count * 128), pl.ds(n, 512)],
+                tokens[:, span], gate_up[span, pl.ds(n, 512)],
                 preferred_element_type=jnp.float32,
             )
-            if c:
+            if c > 2:
                 piece = product[:, pl.ds(n, 512)] + piece
             product[:, pl.ds(n, 512)] = piece
     gate = product[:, :hidden_dim]
@@ -391,48 +432,91 @@
                 sent.at[4], r2_r.at[c], other(a1, -d, 0),
             )
         back_two[0, :, :, cols] = back_one[:, 0, :, cols]
+    def combine(c):
+        r, start, count = CHUNKS[c]
+        cols = columns(start, count)
+        settle(back_two.at[pl.ds(1, SIDE - 1), :, :, cols], r2_r.at[c])
+        results = back_two[:, :, :, cols].reshape(256, count * 128)
+        parts = jnp.dot(weight[r], results, preferred_element_type=jnp.float32)
+        total = parts[:128] + parts[128:256] + parts[256:]
+        total = total.reshape(2, SIDE, 16, count * 128)
+        if c >= LATE:
+            expert_sum[:, cols] = total[0, 0]
+            partial[0, :, :, cols] = total[1].astype(jnp.bfloat16)
+            partial[1, 1:, :, cols] = total[0, 1:].astype(jnp.bfloat16)
+            for d in (2, 1, 3):
+                send(
+                    partial.at[1, d, :, cols], back_three.at[d, :, cols],
+                    sent.at[5], r1_r.at[c], other(ROTATIONS[r][0], -d, 0),
+                )
+                send(
+                    partial.at[0, d, :, cols], from_core.at[d, :, cols],
+                    core_sems.at[5], core_r.at[c], other(ROTATIONS[r][0], -d, 1),
+                )
+            send(
+                partial.at[0, 0, :, cols], from_core.at[0, :, cols],
+                core_sems.at[6], core_r.at[c], sibling,
+            )
+            return
+        near_sum[:, :, cols] = total[0]
+        partial[0, :, :, cols] = total[1].astype(jnp.bfloat16)
+        send(
+            partial.at[0, :, :, cols], from_core.at[:, :, cols],
+            core_sems.at[3], core_r.at[c], sibling,
+        )
+
+    def pass_on(c):
+        r, start, count = CHUNKS[c]
+        cols = columns(start, count)
+        settle(from_core.at[:, :, cols], core_r.at[c])
+        total = near_sum[:, :, cols] + from_core[:, :, cols].astype(jnp.float32)
+        expert_sum[:, cols] = total[0]
+        partial[1, 1:, :, cols] = total[1:].astype(jnp.bfloat16)
+        for d in (2, 1, 3):
+            send(
+                partial.at[1, d, :, cols], back_three.at[d, :, cols],
+                sent.at[5], r1_r.at[c], other(ROTATIONS[r][0], -d, 0),
+            )
+
+    for step in range(len(CHUNKS)):
+        combine(step)
+        if 0 <= step - BEHIND < LATE:
+            pass_on(step - BEHIND)
     for c, (r, start, count) in enumerate(CHUNKS):
-        a0 = ROTATIONS[r][0]
-        settle(back_two.at[pl.ds(1, SIDE - 1), :, :, columns(start, count)], r2_r.at[c])
-        cols = columns(start, count)
-        results = back_two[:, :, :, cols].reshape(256, count * 128)
-        total = None
-        for part in range(3):
-            piece = lax.dot_general(
-                weight[r, part], results, (((0,), (0,)), ((), ())),
-                preferred_element_type=jnp.float32,
-            )
-            total = piece if total is None else total + piece
-        total = total.reshape(PEERS, 16, count * 128)
-        expert_sum[:, cols] = total[0]
-        partial[1:, :, cols] = total[1:].astype(jnp.bfloat16)
-        for s in range(1, PEERS):
-            send(
-                partial.at[s, :, cols], back_three.at[s, :, cols],
-                sent.at[5], r1_r.at[c], other(a0, -(s // 2), s % 2),
-            )
-    for c, (r, start, count) in enumerate(CHUNKS):
-        settle(back_three.at[pl.ds(1, PEERS - 1), :, columns(start, count)], r1_r.at[c])
-        cols = columns(start, count)
+        cols = columns(start, count)
+        settle(back_three.at[pl.ds(1, SIDE - 1), :, cols], r1_r.at[c])
         total = expert_sum[:, cols]
-        for s in range(1, PEERS):
-            total = total + back_three[s, :, cols].astype(jnp.float32)
+        for d in range(1, SIDE):
+            total = total + back_three[d, :, cols].astype(jnp.float32)
+        if c >= LATE:
+            settle(from_core.at[:, :, cols], core_r.at[c])
+            for d in range(SIDE):
+                total = total + from_core[d, :, cols].astype(jnp.float32)
         merged[:, cols] = (merged[:, cols].astype(jnp.float32) + total).astype(jnp.bfloat16)
-    write_layer = pltpu.make_async_copy(merged, layer_out, w_sems.at[5])
-    write_layer.start()
+        pltpu.make_async_copy(merged.at[:, cols], layer_out.at[:, cols], w_sems.at[5]).start()
     settle(shed_list, shed_sems.at[0])
     settle(gathered, code_sems.at[0])
     settle(shed_out, shed_sems.at[2])
+    settle(normed, core_sems.at[0])
+    width = normed.shape[1]
+    early = CHUNKS[EARLY][1] * 128
+    late = CHUNKS[LATE][1] * 128
+    far = pl.ds(SIDE + 1, SIDE - 1)
+    settle(first.at[far, :, pl.ds(early, width - early)], core_sems.at[2])
+    settle(first.at[far, :, pl.ds(0, early)], core_sems.at[4])
+    settle(from_core.at[:, :, pl.ds(0, late)], core_sems.at[3])
+    settle(from_core.at[pl.ds(1, SIDE - 1), :, pl.ds(late, width - late)], core_sems.at[5])
+    settle(from_core.at[0, :, pl.ds(late, width - late)], core_sems.at[6])
     for i, region in enumerate(
         (
-            first.at[pl.ds(1, PEERS - 1)], packed.at[pl.ds(1, SIDE - 1)],
+            first.at[pl.ds(1, SIDE - 1)], packed.at[pl.ds(1, SIDE - 1)],
             third.at[pl.ds(1, SIDE - 1)], sent_back.at[pl.ds(1, SIDE - 1)],
-            back_two.at[pl.ds(1, SIDE - 1)], partial.at[pl.ds(1, PEERS - 1)],
+            back_two.at[pl.ds(1, SIDE - 1)], partial.at[1, pl.ds(1, SIDE - 1)],
         )
     ):
         settle(region, sent.at[i])
     write_attended.wait()
-    write_layer.wait()
+    settle(merged, w_sems.at[5])
 
 
 def local(
@@ -489,21 +573,25 @@
             pltpu.VMEM(down.shape, bf16),
             pltpu.VMEM((19, 16, 128), f32),
             pltpu.VMEM((3, 256, 128), bf16),
-            pltpu.VMEM((3, 3, 256, 128), bf16),
+            pltpu.VMEM((3, 3 * 128, 256), bf16),
             peers,
             block,
             block,
             block,
+            pltpu.VMEM((256, width), bf16),
             pltpu.VMEM((256, 2 * hidden_dim), f32),
             pltpu.VMEM((3, 256, hidden_dim), bf16),
             block,
             block,
             block,
-            peers,
-            peers,
-            dma((6,)), dma((8,)), dma((4,)), dma((2,)), dma((6,)),
+            pltpu.VMEM((2, SIDE, 16, width), bf16),
+            pltpu.VMEM((SIDE, 16, width), f32),
+            pltpu.VMEM((SIDE, 16, width), bf16),
+            pltpu.VMEM((SIDE, 16, width), bf16),
+            dma((6,)), dma((8,)), dma((4,)), dma((2,)), dma((6,)), dma((7,)),
             dma((chunks,)), dma((chunks,)), dma((chunks,)),
             dma((chunks,)), dma((chunks,)), dma((chunks,)),
+            dma((chunks,)), dma((chunks,)),
         ],
         compiler_params=pltpu.CompilerParams(
             collective_id=0, has_side_effects=True, vmem_limit_bytes=52 * 1024 * 1024

time: 74 us -> 70.6 us (0.954)
  Pallas kernels: 72 us -> 68.6 us
    pallas_call x1, Pallas kernels: 72 us -> 68.6 us  [local(): pl.pallas_call(layer_kernel, out_shape=(jax.ShapeDtypeStruct((rows, width...]
where the time goes in v4:
time: 70.6 us; the launch traced here: 70.5 us
  Pallas kernels  68.6 us (97%)
  local copies, waits for them, and re-layouts  1.31 us (2%)
    pallas_call x1, Pallas kernels, local(): pl.pallas_call(layer_kernel, out_shape=(jax.ShapeDtypeStruct((rows, width...  68.6 us

profile of v4, /device:TPU:1, one launch (start us, length us, event | category | flops | bytes accessed | tf_op | source)
XLA Modules:
  0.0 70.5 jit_solution(7524344899513234640)
XLA Ops:
  0.6 68.6 %shard_map.131 = (bf16[16,4096]{1,0:T(8,128)(2,1)S(1)}, bf16[16,4096]{1,0:T(8,128)(2,1)S(1)}) custom-call(bf16[16,4096]{1,0:T(8,128)(2,1)} %queries_hbm.1, bf16[16,512]{1,0:T(8,128)(2,1)} %new_kv_hbm.1, bf16[128,16,512]{2,1,0:T(8,128)(2,1)} %pages_hbm.1, s32[16,16]{1,0:T(8,128)} %page_table_hbm.1, s32[1,16]{1,0:T(1,128)} %bitcast.12, s32[1,16]{1,0:T(1,128)} %bitcast.13, ...), custom_call_target="tpu_custom_call" | custom-call | tf_op jit(solution)/shard_map/pallas_call | solution.py:538
  69.2 0.7 copy.16
  69.9 0.7 copy.17

commit v5 on v4

--- a/solution.py
+++ b/solution.py
@@ -152,12 +152,15 @@
     to_scalar = pltpu.make_async_copy(wanted_list, wanted_scalar, w_sems.at[3])
     to_scalar.start()
     to_scalar.wait()
-    half = shed_out.shape[0] // 2
+    half = shed_out.shape[2] // 2
     for part in range(2):
-        for i in range(part * half, part * half + half):
-            shed_out[i] = pages[wanted_scalar[0, i]]
         span = pl.ds(part * half, half)
-        send(shed_out.at[span], shed_in.at[span], shed_sems.at[2], shed_sems.at[3], partner)
+        for i in range(shed_out.shape[0]):
+            shed_out[i, :, span] = pages[wanted_scalar[0, i], :, span]
+        send(
+            shed_out.at[:, :, span], shed_in.at[:, :, span],
+            shed_sems.at[2], shed_sems.at[3 + part], partner,
+        )
 
     for load in inputs[2:]:
         load.wait()
@@ -278,8 +281,8 @@
 
 
     shed_mask = allowed(float(own_pages))
-    settle(shed_in, shed_sems.at[3])
-    square = jnp.zeros((ROWS, HEAD), f32)
+    settle(shed_in.at[:, :, pl.ds(0, half)], shed_sems.at[3])
+    late_parts = []
     for g in range(GROUPS):
         keys = shed_in[:, :, g * HEAD : (g + 1) * HEAD].reshape(TILE, HEAD)
         values = masked(dot_last(heads[g], keys), shed_mask)
@@ -287,11 +290,16 @@
         again = jnp.exp((tops[g] - top) * scaling)
         weights = jnp.exp((values - top) * scaling)
         denominator = sums[g] * again + jnp.sum(weights, axis=1, keepdims=True)
+        inverse = 1.0 / denominator
+        summed[g] = summed[g] * (again * inverse)
+        late_parts.append((weights.astype(bf16), inverse))
+    settle(shed_in.at[:, :, pl.ds(half, half)], shed_sems.at[4])
+    square = jnp.zeros((ROWS, HEAD), f32)
+    for g in range(GROUPS):
+        weights, inverse = late_parts[g]
         values = shed_in[:, :, (GROUPS + g) * HEAD : (GROUPS + g + 1) * HEAD].reshape(TILE, HEAD)
-        total = summed[g] * again + jnp.dot(
-            weights.astype(bf16), values, preferred_element_type=f32
-        )
-        total = (total / denominator).astype(bf16)
+        total = summed[g] + jnp.dot(weights, values, preferred_element_type=f32) * inverse
+        total = total.astype(bf16)
         for h in range(GROUP_HEADS):
             span = pl.ds((g * GROUP_HEADS + h) * HEAD, HEAD)
             part = total[h * ROWS : (h + 1) * ROWS, :]
@@ -402,16 +410,16 @@
     gate = product[:, :hidden_dim]
     active = (gate / (1.0 + jnp.exp(-gate)) * product[:, hidden_dim:]).astype(jnp.bfloat16)
     hidden[0] = active
-    for r in (1, 2):
-        turned = lax.dot_general(
-            orders[r], active, (((0,), (0,)), ((), ())), preferred_element_type=jnp.float32
-        )
-        hidden[r] = turned.astype(jnp.bfloat16)
 
     loads[1].wait()
     for c, (r, start, count) in enumerate(CHUNKS):
         a2 = ROTATIONS[r][2]
         cols = columns(start, count)
+        if c in (1, 2):
+            turned = lax.dot_general(
+                orders[r], active, (((0,), (0,)), ((), ())), preferred_element_type=jnp.float32
+            )
+            hidden[r] = turned.astype(jnp.bfloat16)
         finished = jnp.dot(hidden[r], down[:, cols], preferred_element_type=jnp.float32)
         finished = finished.astype(jnp.bfloat16).reshape(SIDE, SIDE, 16, count * 128)
         back_one[0, :, :, cols] = finished[0]
@@ -588,7 +596,7 @@
             pltpu.VMEM((SIDE, 16, width), f32),
             pltpu.VMEM((SIDE, 16, width), bf16),
             pltpu.VMEM((SIDE, 16, width), bf16),
-            dma((6,)), dma((8,)), dma((4,)), dma((2,)), dma((6,)), dma((7,)),
+            dma((6,)), dma((8,)), dma((5,)), dma((2,)), dma((6,)), dma((7,)),
             dma((chunks,)), dma((chunks,)), dma((chunks,)),
             dma((chunks,)), dma((chunks,)), dma((chunks,)),
             dma((chunks,)), dma((chunks,)),

time: 70.6 us -> 69.5 us (0.984)
  Pallas kernels: 68.6 us -> 67.5 us
    pallas_call x1, Pallas kernels: 68.6 us -> 67.5 us  [local(): pl.pallas_call(layer_kernel, out_shape=(jax.ShapeDtypeStruct((rows, width...]
where the time goes in v5:
time: 69.5 us; the launch traced here: 69.4 us
  Pallas kernels  67.5 us (97%)
  local copies, waits for them, and re-layouts  1.31 us (2%)
    pallas_call x1, Pallas kernels, local(): pl.pallas_call(layer_kernel, out_shape=(jax.ShapeDtypeStruct((rows, width...  67.5 us

profile of v5, /device:TPU:1, one launch (start us, length us, event | category | flops | bytes accessed | tf_op | source)
XLA Modules:
  0.0 69.4 jit_solution(14214676122032864327)
XLA Ops:
  0.6 67.5 %shard_map.131 = (bf16[16,4096]{1,0:T(8,128)(2,1)S(1)}, bf16[16,4096]{1,0:T(8,128)(2,1)S(1)}) custom-call(bf16[16,4096]{1,0:T(8,128)(2,1)} %queries_hbm.1, bf16[16,512]{1,0:T(8,128)(2,1)} %new_kv_hbm.1, bf16[128,16,512]{2,1,0:T(8,128)(2,1)} %pages_hbm.1, s32[16,16]{1,0:T(8,128)} %page_table_hbm.1, s32[1,16]{1,0:T(1,128)} %bitcast.12, s32[1,16]{1,0:T(1,128)} %bitcast.13, ...), custom_call_target="tpu_custom_call" | custom-call | tf_op jit(solution)/shard_map/pallas_call | solution.py:546
  68.1 0.7 copy.16
  68.8 0.7 copy.17

commit v6 on v5

--- a/solution.py
+++ b/solution.py
@@ -354,7 +354,6 @@
         rows = first[:, :, cols].reshape(PEERS * 16, count * 128)
         block = jnp.dot(select[r], rows, preferred_element_type=jnp.float32).astype(jnp.bfloat16)
         block = block.reshape(SIDE, SIDE, 16, count * 128)
-        second[0, :, :, cols] = block[0]
         for d in (2, 1, 3):
             packed[d, :, :, cols] = block[d]
         for d in (2, 1, 3):
@@ -362,6 +361,7 @@
                 packed.at[d, :, :, cols], second.at[d, :, :, cols],
                 sent.at[1], s2_r.at[c], other(a1, d, 0),
             )
+        second[0, :, :, cols] = block[0]
     for c, (r, start, count) in enumerate(CHUNKS):
         a2 = ROTATIONS[r][2]
         settle(second.at[pl.ds(1, SIDE - 1), :, :, columns(start, count)], s2_r.at[c])
@@ -422,7 +422,6 @@
             hidden[r] = turned.astype(jnp.bfloat16)
         finished = jnp.dot(hidden[r], down[:, cols], preferred_element_type=jnp.float32)
         finished = finished.astype(jnp.bfloat16).reshape(SIDE, SIDE, 16, count * 128)
-        back_one[0, :, :, cols] = finished[0]
         for d in (2, 1, 3):
             sent_back[d, :, :, cols] = finished[d]
         for d in (2, 1, 3):
@@ -430,6 +429,7 @@
                 sent_back.at[d, :, :, cols], back_one.at[d, :, :, cols],
                 sent.at[3], r3_r.at[c], other(a2, -d, 0),
             )
+        back_one[0, :, :, cols] = finished[0]
     for c, (r, start, count) in enumerate(CHUNKS):
         a1 = ROTATIONS[r][1]
         settle(back_one.at[pl.ds(1, SIDE - 1), :, :, columns(start, count)], r3_r.at[c])

time: 69.5 us -> 69.9 us (level)
  no operation moved by 1% of the time
where the time goes in v6:
time: 69.9 us; the launch traced here: 69.8 us
  Pallas kernels  67.9 us (97%)
  local copies, waits for them, and re-layouts  1.31 us (2%)
    pallas_call x1, Pallas kernels, local(): pl.pallas_call(layer_kernel, out_shape=(jax.ShapeDtypeStruct((rows, width...  67.9 us

profile of v6, /device:TPU:1, one launch (start us, length us, event | category | flops | bytes accessed | tf_op | source)
XLA Modules:
  0.0 69.8 jit_solution(4885338992469761533)
XLA Ops:
  0.6 67.9 %shard_map.131 = (bf16[16,4096]{1,0:T(8,128)(2,1)S(1)}, bf16[16,4096]{1,0:T(8,128)(2,1)S(1)}) custom-call(bf16[16,4096]{1,0:T(8,128)(2,1)} %queries_hbm.1, bf16[16,512]{1,0:T(8,128)(2,1)} %new_kv_hbm.1, bf16[128,16,512]{2,1,0:T(8,128)(2,1)} %pages_hbm.1, s32[16,16]{1,0:T(8,128)} %page_table_hbm.1, s32[1,16]{1,0:T(1,128)} %bitcast.12, s32[1,16]{1,0:T(1,128)} %bitcast.13, ...), custom_call_target="tpu_custom_call" | custom-call | tf_op jit(solution)/shard_map/pallas_call | solution.py:546
  68.5 0.7 copy.16
  69.2 0.7 copy.17
